TPU v7x, 32 devices: a whole 2x2x4 slice. The times are simulated.
32 devices in a mesh: req: 16 (over z, y, x), tp: 2 (over core).
Axes of the slice: x: 2, y: 2, z: 4, core: 2. Of those that a mesh axis runs over, the one named last changes fastest.
Arguments:
- attn: bfloat16 [2048, 2048], P('req', 'tp'), may hold values from -6 to 6
- out_weight: bfloat16 [2048, 2048], P('tp'), may hold values from -0.125 to 0.125
- stream_in: bfloat16 [2048, 2048], P(('req', 'tp')), may hold values from -12 to 12
- norm_gain: float32 [2048], replicated, may hold values from 0.5 to 1.5
- router_weight: bfloat16 [2048, 32], replicated, may hold values from -0.024902344 to 0.024902344
- routes: int32 [2048, 8], P(('req', 'tp')), may hold values from 0 to 31, all different within a row; in each aligned block of 64 rows (0 to 63, 64 to 127, ...) at most 32 rows name the same one
- gate_weight: bfloat16 [32, 1024, 2048], P('req', 'tp'), may hold values from -0.125 to 0.125
- up_weight: bfloat16 [32, 1024, 2048], P('req', 'tp'), may hold values from -0.125 to 0.125
- down_weight: bfloat16 [32, 1024, 2048], P('req', 'tp'), may hold values from -0.1875 to 0.1875
Outputs:
- stream: bfloat16 [2048, 2048], P(('req', 'tp'))
- expert_mix: bfloat16 [2048, 2048], P(('req', 'tp'))
Inputs may be any that keep to these rules, and one draw needn't show every extreme that they name: `routes`: each row names 8 different experts; among the rows of one aligned block of 64 rows no expert is named by more than 32 rows, and some expert reaches 32 in some block.
All inputs are finite; a program needn't handle non-finite values.
Results may differ from a plain program's by a relative error of at most 0.009.
Values may be sent and summed in bfloat16 or wider, within the bound.
No kernel may reach another device: no remote copies, remote signals or barrier semaphores. Data moves between devices by JAX's collectives and lax.ppermute only.
A program may use at most 128 MiB of HBM per device.

v0:
```python
import functools

import jax
import jax.numpy as jnp
from jax import lax
from jax.experimental import pallas as pl
from jax.experimental.pallas import tpu as pltpu
from jax.sharding import PartitionSpec as P

SWAP = [(0, 1), (1, 0)]
PLACES = 16
ACROSS_X = [(2 * i + t, 2 * (i ^ (1 + t)) + t) for i in range(PLACES) for t in range(2)]
ACROSS_Y = [(2 * i + t, 2 * (i ^ (2 - t)) + t) for i in range(PLACES) for t in range(2)]


def along_z(places):
    return [(2 * i + t, 2 * j + t) for i, j in places for t in range(2)]


PAIR_Z = along_z([(i, i ^ 4) for i in range(PLACES)])
MIDDLE_Z = along_z([(i, i ^ 12) for i in range(4, 12)])
OPPOSITE_Z = along_z([(i, i ^ 12) for i in range(PLACES)])
INWARD_Z = along_z([(i, i ^ 4) for i in (0, 1, 2, 3, 12, 13, 14, 15)])
OUTWARD_Z = along_z([(i, i ^ 4) for i in range(4, 12)])
NT = (((1,), (1,)), ((), ()))


def send(value, pairs):
    return lax.ppermute(value, ("req", "tp"), pairs)


def wide(value):
    return value.astype(jnp.float32)


def narrow(value):
    return value.astype(jnp.bfloat16)


def joined(*parts):
    return jnp.concatenate(parts, axis=0)


def together(*values):
    return lax.optimization_barrier(values)


def spread(own, weights):
    rows = own.shape[0]
    half = rows // 2
    z = lax.axis_index("req") // 4
    middle = (z == 1) | (z == 2)
    swapped = []

    def swap(value):
        swapped.append(lax.ppermute(value, "tp", SWAP))

    gate_w, up_w, down_w = weights
    swap(gate_w)
    own, up_w, swapped[0] = together(own, up_w, swapped[0])
    over = send(own, OPPOSITE_Z)
    pair = send(own, PAIR_Z)
    x0 = send(own, ACROSS_X)
    y0 = send(own, ACROSS_Y)
    swap(up_w)
    over, pair, x0, y0, swapped[1] = together(over, pair, x0, y0, swapped[1])
    to_x = joined(pair, y0[:half])
    to_y = joined(pair, x0[half:])
    over, pair, to_x, to_y, down_w = together(over, pair, to_x, to_y, down_w)
    out = send(over, OUTWARD_Z)
    next_ = send(pair, MIDDLE_Z)
    x1 = send(to_x, ACROSS_X)
    y1 = send(to_y, ACROSS_Y)
    swap(down_w)
    out, next_, x1, y1, swapped[2] = together(out, next_, x1, y1, swapped[2])
    far1 = jnp.where(middle, over, out)
    far2 = jnp.where(middle, next_, over)
    to_x = joined(far1, far2, y1[:half])
    to_y = joined(far1, far2, x1[half:rows])
    far1, far2, to_x, to_y = together(far1, far2, to_x, to_y)
    x2 = send(to_x, ACROSS_X)
    y2 = send(to_y, ACROSS_Y)
    return [own, x0, y0, pair, x1, y1], far1, far2, x2, y2, swapped


def spread_last(x2, y2, rows):
    half = rows // 2
    to_x = joined(y2[:half], y2[rows : rows + half])
    to_y = joined(x2[half:rows], x2[rows + half : 2 * rows])
    to_x, to_y = together(to_x, to_y)
    return send(to_x, ACROSS_X), send(to_y, ACROSS_Y)


def collect(first, second):
    own, x0, y0, pair, x1, y1 = first
    far1, far2, x_far1, x_far2, y_far1, y_far2, x3, y3 = second
    rows = own.shape[0]
    half = rows // 2

    def low(value, term):
        return joined(narrow(wide(value[:half]) + wide(term)), value[half:])

    def high(value, term):
        return joined(
            value[:half], narrow(wide(value[half:rows]) + wide(term)), value[rows:]
        )

    by_x = send(x3, ACROSS_X)
    by_y = send(y3, ACROSS_Y)
    x_sum = send(high(x_far2, by_y[half:]), ACROSS_X)
    y_sum = send(low(y_far2, by_x[half:]), ACROSS_Y)
    z = lax.axis_index("req") // 4
    middle = (z == 1) | (z == 2)
    far2 = wide(far2) + wide(x_sum) + wide(y_sum)
    next_ = send(narrow(far2), MIDDLE_Z)
    x_sum = send(high(x_far1, by_y[:half]), ACROSS_X)
    y_sum = send(low(y_far1, by_x[:half]), ACROSS_Y)
    far1 = wide(far1) + wide(x_sum[:rows]) + wide(y_sum[:rows])
    inward = send(narrow(far1), INWARD_Z)
    over = send(narrow(jnp.where(middle, far1 + wide(inward), far2)), OPPOSITE_Z)
    x_pair = send(high(x1, y_sum[rows:]), ACROSS_X)
    y_pair = send(low(y1, x_sum[rows:]), ACROSS_Y)
    pair = wide(pair) + wide(x_pair[:rows]) + wide(y_pair[:rows])
    by_pair = send(narrow(pair + wide(next_)), PAIR_Z)
    x_own = send(high(x0, y_pair[rows:]), ACROSS_X)
    y_own = send(low(y0, x_pair[rows:]), ACROSS_Y)
    total = wide(own) + wide(x_own) + wide(y_own)
    return total + wide(over) + wide(by_pair)


def expert_body(takes, gives, tile, group, *refs):
    pieces = len({i for i, _, _ in takes})
    blocks = refs[:pieces]
    router, local, gate_own, up_own, down_own, gate_far, up_far, down_far = refs[
        pieces : pieces + 8
    ]
    outs = refs[pieces + 8 : pieces + 8 + len(gives)]
    held, picks, spreads, sel, acts, ups, downs, up_sem, down_sem = refs[
        pieces + 8 + len(gives) :
    ]
    total_rows, width = held.shape
    experts = router.shape[1]
    tiles = acts.shape[1]
    groups = total_rows // group
    slots = group // 2

    def up_copies(t):
        part = pl.ds(pl.multiple_of(t * tile, tile), tile)
        return [
            pltpu.make_async_copy(w.at[part, :], ups.at[i, t], up_sem.at[i, t])
            for i, w in enumerate((gate_own, up_own, gate_far, up_far))
        ]

    def down_copy(i):
        return pltpu.make_async_copy(
            (down_own, down_far)[i], downs.at[i], down_sem.at[i]
        )

    for t in range(min(2, tiles)):
        for copy in up_copies(t):
            copy.start()
    at = 0
    for i, start, size in takes:
        held[at : at + size, :] = blocks[i][start : start + size, :width]
        picks[at : at + size, :] = blocks[i][start : start + size, width : width + 128]
        at += size
    for g in range(groups):
        part = slice(g * group, (g + 1) * group)
        x = held[part, :]
        pick = picks[part, :experts].astype(jnp.float32)
        logits = jnp.dot(x, router[...], preferred_element_type=jnp.float32)
        raised = jnp.where(pick > 0, jnp.exp(logits), 0.0)
        gate = raised / jnp.sum(raised, axis=1, keepdims=True)
        row = lax.broadcasted_iota(jnp.int32, (group, 1), 0)
        column = lax.broadcasted_iota(jnp.int32, (group, group), 1)
        chosen = jnp.zeros((group, group), jnp.float32)
        weighed = jnp.zeros((group, group), jnp.float32)
        for j in range(2):
            mine = local[j : j + 1, :]
            slot = jnp.sum(pick * mine, axis=1, keepdims=True).astype(jnp.int32)
            place = jnp.where(slot > 0, j * slots + row // 64 * 32 + slot - 1, -1)
            weight = jnp.sum(gate * mine, axis=1, keepdims=True)
            hit = column == place
            chosen = jnp.where(hit, 1.0, chosen)
            weighed = jnp.where(hit, weight, weighed)
        spreads[g] = weighed.astype(jnp.bfloat16)
        rows = jnp.dot(
            chosen.T.astype(jnp.bfloat16), x, preferred_element_type=jnp.float32
        ).astype(jnp.bfloat16)
        for j in range(2):
            sel[j, g * slots : (g + 1) * slots, :] = rows[j * slots : (j + 1) * slots, :]

    def up(t, _):
        @pl.when(t + 2 < tiles)
        def _():
            for copy in up_copies(t + 2):
                copy.start()

        @pl.when(t + 2 == tiles)
        def _():
            for i in range(2):
                down_copy(i).start()

        for copy in up_copies(t):
            copy.wait()
        x = sel[t // (tiles // 2)]
        for i in range(2):
            h = lax.dot_general(x, ups[2 * i, t], NT, preferred_element_type=jnp.float32)
            u = lax.dot_general(
                x, ups[2 * i + 1, t], NT, preferred_element_type=jnp.float32
            )
            acts[i, t] = (h / (1.0 + jnp.exp(-h)) * u).astype(jnp.bfloat16)
        return 0

    lax.fori_loop(0, tiles, up, 0)
    for i in range(2):
        down_copy(i).wait()

    def down(n, _):
        part = pl.ds(pl.multiple_of(n * tile, tile), tile)
        rows = []
        for j in range(2):
            total = None
            for t in range(j * tiles // 2, (j + 1) * tiles // 2):
                for i in range(2):
                    term = jnp.dot(
                        acts[i, t],
                        downs[i, t * tile : (t + 1) * tile, part],
                        preferred_element_type=jnp.float32,
                    )
                    total = term if total is None else total + term
            rows.append(total.astype(jnp.bfloat16))
        mixed = []
        for g in range(groups):
            slot_rows = jnp.concatenate(
                [r[g * slots : (g + 1) * slots, :] for r in rows], axis=0
            )
            mixed.append(
                jnp.dot(spreads[g], slot_rows, preferred_element_type=jnp.float32).astype(
                    jnp.bfloat16
                )
            )
        for out, ranges in zip(outs, gives):
            at = 0
            for start, size in ranges:
                g = start // group
                out[at : at + size, part] = mixed[g][start - g * group : start - g * group + size, :]
                at += size
        return 0

    lax.fori_loop(0, width // tile, down, 0)


def run_experts(blocks, takes, gives, router, local, own, far, tile=256, group=256):
    width = router.shape[0]
    hidden = own[0].shape[0]
    total_rows = sum(size for _, _, size in takes)
    sizes = [sum(size for _, size in ranges) for ranges in gives]
    vmem = pl.BlockSpec(memory_space=pltpu.VMEM)
    return pl.pallas_call(
        functools.partial(expert_body, takes, gives, tile, group),
        in_specs=[vmem] * (len(blocks) + 2) + [pl.BlockSpec(memory_space=pl.ANY)] * 6,
        out_specs=[vmem] * len(sizes),
        out_shape=[jax.ShapeDtypeStruct((size, width), jnp.bfloat16) for size in sizes],
        scratch_shapes=[
            pltpu.VMEM((total_rows, width), jnp.bfloat16),
            pltpu.VMEM((total_rows, 128), jnp.bfloat16),
            pltpu.VMEM((total_rows // group, group, group), jnp.bfloat16),
            pltpu.VMEM((2, total_rows // 2, width), jnp.bfloat16),
            pltpu.VMEM((2, hidden // tile, total_rows // 2, tile), jnp.bfloat16),
            pltpu.VMEM((4, hidden // tile, tile, width), jnp.bfloat16),
            pltpu.VMEM((2, hidden, width), jnp.bfloat16),
            pltpu.SemaphoreType.DMA((4, hidden // tile)),
            pltpu.SemaphoreType.DMA((2,)),
        ],
        compiler_params=pltpu.CompilerParams(vmem_limit_bytes=42 * 1024 * 1024),
        cost_estimate=pl.CostEstimate(
            flops=8 * total_rows * width * hidden,
            bytes_accessed=12 * hidden * width + 4 * total_rows * width,
            transcendentals=total_rows * hidden,
        ),
    )(*blocks, router, local, *own, *far)


def project(attn, out_weight, stream_in, later):
    rows = stream_in.shape[0]
    me = lax.axis_index("tp")
    theirs = lax.dynamic_slice_in_dim(attn, (1 - me) * rows, rows, 0)
    ours = lax.dynamic_slice_in_dim(attn, me * rows, rows, 0)
    sent = jnp.dot(theirs, out_weight, preferred_element_type=jnp.float32)
    got = lax.ppermute(sent, "tp", SWAP)
    kept = jnp.dot(ours, out_weight, preferred_element_type=jnp.float32)
    got, later = lax.optimization_barrier((got, later))
    return stream_in.astype(jnp.float32) + (kept + got), later


def on_places(
    attn, out_weight, stream_in, norm_gain, router_weight, routes, gate_weight, up_weight, down_weight
):
    rows = stream_in.shape[0]
    half = rows // 2
    expert_count = router_weight.shape[1]
    experts = jnp.arange(expert_count, dtype=jnp.int32)
    me = lax.axis_index("req")
    named = jnp.any(routes[:, :, None] == experts, axis=1).astype(jnp.bfloat16)
    order = jnp.arange(rows)
    earlier = (order[None, :] <= order[:, None]).astype(jnp.bfloat16)
    slot = jnp.dot(earlier, named, preferred_element_type=jnp.float32)
    slot = (slot * named).astype(jnp.bfloat16)
    slot = jnp.pad(slot, ((0, 0), (0, 128 - expert_count)))
    local = (experts[None, :] == 2 * me + jnp.arange(2, dtype=jnp.int32)[:, None]).astype(
        jnp.float32
    )
    hidden_state, gate_weight = project(attn, out_weight, stream_in, gate_weight)
    scale = lax.rsqrt(jnp.mean(hidden_state * hidden_state, axis=1, keepdims=True) + 1e-06)
    normed = (hidden_state * scale * norm_gain).astype(jnp.bfloat16)
    width = stream_in.shape[1]
    weights = (gate_weight, up_weight, down_weight)
    own = tuple(w.reshape(-1, width) for w in weights)
    first, far1, far2, x2, y2, far = spread(jnp.concatenate([normed, slot], axis=1), weights)
    far = tuple(w.reshape(-1, width) for w in far)
    run = functools.partial(run_experts, router=router_weight, local=local, own=own, far=far)
    takes = tuple((i, 0, rows) for i in range(7)) + ((4, rows, half), (5, rows, half))
    gives = tuple(((i * rows, rows),) for i in range(4))
    gives += (((4 * rows, rows), (7 * rows, half)),)
    gives += (((5 * rows, rows), (7 * rows + half, half)),)
    gives += (((6 * rows, rows),),)
    done = run(first + [far1], takes, gives)
    x2, y2, *done = lax.optimization_barrier((x2, y2, *done))
    x3, y3 = spread_last(x2, y2, rows)
    first, (far1,) = done[:6], done[6:]
    takes = ((0, 0, 2 * rows), (1, 0, 2 * rows), (0, 2 * rows, half), (1, 2 * rows, half))
    takes += ((2, 0, half), (3, 0, half), (2, half, half), (3, half, half), (4, 0, rows))
    gives = (
        ((0, rows), (4 * rows, half)),
        ((rows, rows),),
        ((2 * rows, rows), (4 * rows + half, half)),
        ((3 * rows, rows),),
        ((5 * rows, half), (6 * rows, half)),
        ((5 * rows + half, half), (6 * rows + half, half)),
        ((7 * rows, rows),),
    )
    *second, far2 = run([x2, y2, x3, y3, far2], takes, gives)
    second = [far1, far2, *second]
    mix = collect(first, second)
    return (hidden_state.astype(jnp.bfloat16), mix.astype(jnp.bfloat16))


def slot_numbers(flat, count):
    onehot = (flat[:, None] == jnp.arange(count, dtype=jnp.int32)[None, :]).astype(jnp.int32)
    before = jnp.cumsum(onehot, axis=0) - onehot
    return jnp.sum(before * onehot, axis=1)


def swiglu_part(rows_in, gate_w, up_w, down_w):
    gate_h = jnp.einsum("ekd,efd->ekf", rows_in, gate_w, preferred_element_type=jnp.float32)
    up_h = jnp.einsum("ekd,efd->ekf", rows_in, up_w, preferred_element_type=jnp.float32)
    act = (jax.nn.silu(gate_h) * up_h).astype(jnp.bfloat16)
    return jnp.einsum("ekf,efd->ekd", act, down_w, preferred_element_type=jnp.float32)


def on_slots(
    attn, out_weight, stream_in, norm_gain, router_weight, routes, gate_weight, up_weight, down_weight
):
    rows, width = stream_in.shape
    hidden_state, _ = project(attn, out_weight, stream_in, gate_weight)
    scale = lax.rsqrt(jnp.mean(hidden_state * hidden_state, axis=1, keepdims=True) + 1e-06)
    normed = (hidden_state * scale * norm_gain).astype(jnp.bfloat16)
    expert_count = router_weight.shape[1]
    choose_count = routes.shape[1]
    local_experts = gate_weight.shape[0]
    req_count = lax.axis_size("req")
    capacity = 2 * rows * choose_count // expert_count
    logits = jnp.dot(normed, router_weight, preferred_element_type=jnp.float32)
    onehot = (
        routes[:, :, None] == jnp.arange(expert_count, dtype=jnp.int32)[None, None, :]
    ).astype(jnp.float32)
    picked = jnp.sum(onehot * logits[:, None, :], axis=2)
    raised = jnp.exp(picked)
    gates = raised / jnp.sum(raised, axis=1, keepdims=True)
    flat = routes.reshape(-1)
    slots = slot_numbers(flat, expert_count)
    position = (
        flat % local_experts * (req_count * capacity) + flat // local_experts * capacity + slots
    )
    source = jnp.arange(rows * choose_count, dtype=jnp.int32) // choose_count
    outgoing = (
        jnp.zeros((local_experts * req_count * capacity, width), jnp.bfloat16)
        .at[position]
        .set(normed[source])
    )
    outgoing = outgoing.reshape(local_experts, req_count * capacity, width)
    incoming = lax.all_to_all(outgoing, "req", split_axis=1, concat_axis=1, tiled=True)
    partial_out = swiglu_part(
        lax.all_gather(incoming, "tp", axis=1, tiled=True), gate_weight, up_weight, down_weight
    )
    expert_out = lax.psum_scatter(partial_out, "tp", scatter_dimension=1, tiled=True).astype(
        jnp.bfloat16
    )
    returned = lax.all_to_all(expert_out, "req", split_axis=1, concat_axis=1, tiled=True)
    expert_row = returned.reshape(-1, width)[position].reshape(rows, choose_count, width)
    mix = jnp.einsum("rk,rkd->rd", gates, expert_row.astype(jnp.float32))
    return (hidden_state.astype(jnp.bfloat16), mix.astype(jnp.bfloat16))


def solution(mesh):
    body = on_places if mesh.shape["req"] == PLACES else on_slots
    return jax.shard_map(
        body,
        mesh=mesh,
        in_specs=(
            P("req", "tp"),
            P("tp", None),
            P(("req", "tp"), None),
            P(),
            P(),
            P(("req", "tp"), None),
            P("req", "tp", None),
            P("req", "tp", None),
            P("req", "tp", None),
        ),
        out_specs=(P(("req", "tp"), None), P(("req", "tp"), None)),
        check_vma=False,
    )
```

profile of v0, /device:TPU:0, one launch (start us, length us, event | category | flops | bytes accessed | tf_op | source)
XLA Modules:
  0.0 140.6 jit_solution(9507125580018658170)
XLA Ops:
  1.6 3.1 %fusion.5 = f32[64,2048]{1,0:T(8,128)S(1)} fusion(bf16[1024,2048]{1,0:T(8,128)(2,1)} %param.10, bf16[128,1024]{1,0:T(8,128)(2,1)S(1)} %copy-done, s32[]{:T(128)S(6)} %select_n.33), kind=kOutput, calls=%fused_computation.41 | convolution fusion | flops 268435456 | bytes 4849668 | tf_op jit(solution)/shard_map/dot_general | solution.py:290
  5.2 1.5 %collective-permute-done = f32[64,2048]{1,0:T(8,128)S(1)} collective-permute-done((f32[64,2048]{1,0:T(8,128)S(1)}, f32[64,2048]{1,0:T(8,128)S(1)}, u32[]{:S(2)}, u32[]{:S(2)}) %collective-permute-start) | collective-permute-done | bytes 524320 | tf_op jit(solution)/shard_map/ppermute | solution.py:291
  7.4 3.2 %fusion.7 = f32[64,2048]{1,0:T(8,128)S(1)} fusion(bf16[1024,2048]{1,0:T(8,128)(2,1)} %param.10, bf16[128,1024]{1,0:T(8,128)(2,1)S(1)} %copy-done, s32[]{:T(128)S(6)} %select_n.32), kind=kOutput, calls=%fused_computation.43 | convolution fusion | flops 268435456 | bytes 4849668 | tf_op jit(solution)/shard_map/dot_general | solution.py:292
  11.6 2.7 %collective-permute-done.1 = bf16[2,512,2048]{2,1,0:T(8,128)(2,1)} collective-permute-done((bf16[2,512,2048]{2,1,0:T(8,128)(2,1)}, bf16[2,512,2048]{2,1,0:T(8,128)(2,1)}, u32[]{:S(2)}, u32[]{:S(2)}) %collective-permute-start.1) | collective-permute-done | bytes 4194336 | tf_op jit(solution)/shard_map/ppermute | solution.py:56
  14.6 4.7 %collective-permute-start.2 = (bf16[64,2176]{1,0:T(8,128)(2,1)S(1)}, bf16[64,2176]{1,0:T(8,128)(2,1)S(1)}, u32[]{:S(2)}, u32[]{:S(2)}) collective-permute-start(bf16[64,2176]{1,0:T(8,128)(2,1)S(1)} %fusion.4.refs_0_), channel_id=1, source_target_pairs={{0,24},{1,25},{2,26},{3,27},{4,28},{5,29},{6,30},{7,31},{8,16},{9,... | collective-permute-start | bytes 835592 | tf_op jit(solution)/shard_map/ppermute | solution.py:29
  19.4 1.5 %collective-permute-start.4 = (bf16[64,2176]{1,0:T(8,128)(2,1)S(1)}, bf16[64,2176]{1,0:T(8,128)(2,1)S(1)}, u32[]{:S(2)}, u32[]{:S(2)}) collective-permute-start(bf16[64,2176]{1,0:T(8,128)(2,1)S(1)} %fusion.4.refs_0_), channel_id=1, source_target_pairs={{0,2},{1,5},{2,0},{3,7},{4,6},{5,1},{6,4},{7,3},{8,10},{9,13},{10,... | collective-permute-start | bytes 835592 | tf_op jit(solution)/shard_map/ppermute | solution.py:29
  20.9 1.5 %collective-permute-start.5 = (bf16[64,2176]{1,0:T(8,128)(2,1)S(1)}, bf16[64,2176]{1,0:T(8,128)(2,1)S(1)}, u32[]{:S(2)}, u32[]{:S(2)}) collective-permute-start(bf16[64,2176]{1,0:T(8,128)(2,1)S(1)} %fusion.4.refs_0_), channel_id=1, source_target_pairs={{0,4},{1,3},{2,6},{3,1},{4,0},{5,7},{6,2},{7,5},{8,12},{9,11},{10,... | collective-permute-start | bytes 835592 | tf_op jit(solution)/shard_map/ppermute | solution.py:29
  22.4 4.6 %collective-permute-done.2 = bf16[64,2176]{1,0:T(8,128)(2,1)S(1)} collective-permute-done((bf16[64,2176]{1,0:T(8,128)(2,1)S(1)}, bf16[64,2176]{1,0:T(8,128)(2,1)S(1)}, u32[]{:S(2)}, u32[]{:S(2)}) %collective-permute-start.2) | collective-permute-done | bytes 278560 | tf_op jit(solution)/shard_map/ppermute | solution.py:29
  26.9 5.7 %collective-permute-done.3.refs_3_ = bf16[64,2176]{1,0:T(8,128)(2,1)S(1)} collective-permute-done((bf16[64,2176]{1,0:T(8,128)(2,1)S(1)}, bf16[64,2176]{1,0:T(8,128)(2,1)S(1)}, u32[]{:S(2)}, u32[]{:S(2)}) %collective-permute-start.3) | collective-permute-done | bytes 278560 | tf_op jit(solution)/shard_map/ppermute | solution.py:29
  33.5 1.5 %collective-permute-start.9 = (bf16[96,2176]{1,0:T(8,128)(2,1)}, bf16[96,2176]{1,0:T(8,128)(2,1)S(1)}, u32[]{:S(2)}, u32[]{:S(2)}) collective-permute-start(bf16[96,2176]{1,0:T(8,128)(2,1)} %get-tuple-element.61), channel_id=1, source_target_pairs={{0,2},{1,5},{2,0},{3,7},{4,6},{5,1},{6,4},{7,3},{8,10},{9,13},{10,... | collective-permute-start | bytes 1253384 | tf_op jit(solution)/shard_map/ppermute | solution.py:29
  35.0 1.5 %collective-permute-start.10 = (bf16[96,2176]{1,0:T(8,128)(2,1)S(1)}, bf16[96,2176]{1,0:T(8,128)(2,1)S(1)}, u32[]{:S(2)}, u32[]{:S(2)}) collective-permute-start(bf16[96,2176]{1,0:T(8,128)(2,1)S(1)} %get-tuple-element.62), channel_id=1, source_target_pairs={{0,4},{1,3},{2,6},{3,1},{4,0},{5,7},{6,2},{7,5},{8,12},{9,11},{10,... | collective-permute-start | bytes 1253384 | tf_op jit(solution)/shard_map/ppermute | solution.py:29
  36.5 1.3 collective-permute-start.7
  37.8 1.4 collective-permute-start.8
  39.2 1.2 copy.21.refs_7_.refs_5_
  40.5 6.5 %collective-permute-done.7 = bf16[64,2176]{1,0:T(8,128)(2,1)} collective-permute-done((bf16[64,2176]{1,0:T(8,128)(2,1)S(1)}, bf16[64,2176]{1,0:T(8,128)(2,1)}, u32[]{:S(2)}, u32[]{:S(2)}) %collective-permute-start.7) | collective-permute-done | bytes 278560 | tf_op jit(solution)/shard_map/ppermute | solution.py:29
  48.8 1.2 collective-permute-start.13
  50.0 15.1 %shard_map.104 = (bf16[64,2048]{1,0:T(8,128)(2,1)S(1)}, bf16[64,2048]{1,0:T(8,128)(2,1)S(1)}, bf16[64,2048]{1,0:T(8,128)(2,1)S(1)}, bf16[64,2048]{1,0:T(8,128)(2...) custom-call(bf16[64,2176]{1,0:T(8,128)(2,1)S(1)} %fusion.4.refs_0_, ...), custom_call_target="tpu_custom_call" | custom-call | flops 8589934592 | bytes 29360128 | tf_op jit(solution)/shard_map/pallas_call | solution.py:260
  65.7 1.5 %collective-permute-start.14 = (bf16[64,2176]{1,0:T(8,128)(2,1)S(1)}, bf16[64,2176]{1,0:T(8,128)(2,1)S(1)}, u32[]{:S(2)}, u32[]{:S(2)}) collective-permute-start(bf16[64,2176]{1,0:T(8,128)(2,1)S(1)} %pad_maximum_fusion.9), channel_id=1, source_target_pairs={{0,2},{1,5},{2,0},{3,7},{4,6},{5,1},{6,4},{7,3},{8,10},{9,13},{10,... | collective-permute-start | bytes 835592 | tf_op jit(solution)/shard_map/ppermute | solution.py:29
  67.2 1.2 collective-permute-start.15
  68.5 6.8 %collective-permute-done.14.refs_2_ = bf16[64,2176]{1,0:T(8,128)(2,1)S(1)} collective-permute-done((bf16[64,2176]{1,0:T(8,128)(2,1)S(1)}, bf16[64,2176]{1,0:T(8,128)(2,1)S(1)}, u32[]{:S(2)}, u32[]{:S(2)}) %collective-permute-start.14) | collective-permute-done | bytes 278560 | tf_op jit(solution)/shard_map/ppermute | solution.py:29
  75.3 15.2 %shard_map.105 = (bf16[96,2048]{1,0:T(8,128)(2,1)S(1)}, bf16[64,2048]{1,0:T(8,128)(2,1)S(1)}, bf16[96,2048]{1,0:T(8,128)(2,1)S(1)}, bf16[64,2048]{1,0:T(8,128)(2...) custom-call(bf16[160,2176]{1,0:T(8,128)(2,1)S(1)} %collective-permute-done.12.refs, ...), custom_call_target="tpu_custom_call" | custom-call | flops 8589934592 | bytes 29360128 | tf_op jit(solution)/shard_map/pallas_call | solution.py:260
  90.5 1.3 collective-permute-start.20
  92.6 6.3 %collective-permute-done.20 = bf16[64,2048]{1,0:T(8,128)(2,1)S(1)} collective-permute-done((bf16[64,2048]{1,0:T(8,128)(2,1)S(1)}, bf16[64,2048]{1,0:T(8,128)(2,1)S(1)}, u32[]{:S(2)}, u32[]{:S(2)}) %collective-permute-start.20) | collective-permute-done | bytes 262176 | tf_op jit(solution)/shard_map/ppermute | solution.py:29
  100.0 2.1 %collective-permute-start.17 = (bf16[96,2048]{1,0:T(8,128)(2,1)S(1)}, bf16[96,2048]{1,0:T(8,128)(2,1)S(1)}, u32[]{:S(2)}, u32[]{:S(2)}) collective-permute-start(bf16[96,2048]{1,0:T(8,128)(2,1)S(1)} %pad_maximum_fusion.5), channel_id=1, source_target_pairs={{0,2},{1,5},{2,0},{3,7},{4,6},{5,1},{6,4},{7,3},{8,10},{9,13},{10,... | collective-permute-start | bytes 1179656 | tf_op jit(solution)/shard_map/ppermute | solution.py:29
  103.5 7.7 %collective-permute-done.21 = bf16[96,2048]{1,0:T(8,128)(2,1)S(1)} collective-permute-done((bf16[96,2048]{1,0:T(8,128)(2,1)S(1)}, bf16[96,2048]{1,0:T(8,128)(2,1)S(1)}, u32[]{:S(2)}, u32[]{:S(2)}) %collective-permute-start.21) | collective-permute-done | bytes 393248 | tf_op jit(solution)/shard_map/ppermute | solution.py:29
  111.2 4.3 %collective-permute-start.24 = (bf16[64,2048]{1,0:T(8,128)(2,1)S(1)}, bf16[64,2048]{1,0:T(8,128)(2,1)S(1)}, u32[]{:S(2)}, u32[]{:S(2)}) collective-permute-start(bf16[64,2048]{1,0:T(8,128)(2,1)S(1)} %fusion.2), channel_id=1, source_target_pairs={{0,8},{1,9},{2,10},{3,11},{4,12},{5,13},{6,14},{7,15},{24,16},{25,... | collective-permute-start | bytes 786440 | tf_op jit(solution)/shard_map/ppermute | solution.py:29
  115.6 1.8 %collective-permute-start.18 = (bf16[96,2048]{1,0:T(8,128)(2,1)S(1)}, bf16[96,2048]{1,0:T(8,128)(2,1)S(1)}, u32[]{:S(2)}, u32[]{:S(2)}) collective-permute-start(bf16[96,2048]{1,0:T(8,128)(2,1)S(1)} %pad_maximum_fusion.6), channel_id=1, source_target_pairs={{0,4},{1,3},{2,6},{3,1},{4,0},{5,7},{6,2},{7,5},{8,12},{9,11},{10,... | collective-permute-start | bytes 1179656 | tf_op jit(solution)/shard_map/ppermute | solution.py:29
  120.4 1.9 %collective-permute-start.27 = (bf16[64,2048]{1,0:T(8,128)(2,1)S(1)}, bf16[64,2048]{1,0:T(8,128)(2,1)S(1)}, u32[]{:S(2)}, u32[]{:S(2)}) collective-permute-start(bf16[64,2048]{1,0:T(8,128)(2,1)S(1)} %get-tuple-element.102), channel_id=1, source_target_pairs={{0,24},{1,25},{2,26},{3,27},{4,28},{5,29},{6,30},{7,31},{8,16},{9,... | collective-permute-start | bytes 786440 | tf_op jit(solution)/shard_map/ppermute | solution.py:29
  122.3 3.0 %collective-permute-done.22 = bf16[96,2048]{1,0:T(8,128)(2,1)S(1)} collective-permute-done((bf16[96,2048]{1,0:T(8,128)(2,1)S(1)}, bf16[96,2048]{1,0:T(8,128)(2,1)S(1)}, u32[]{:S(2)}, u32[]{:S(2)}) %collective-permute-start.22) | collective-permute-done | bytes 393248 | tf_op jit(solution)/shard_map/ppermute | solution.py:29
  125.4 1.2 collective-permute-start.23
  127.1 8.1 %collective-permute-start.29 = (bf16[64,2048]{1,0:T(8,128)(2,1)S(1)}, bf16[64,2048]{1,0:T(8,128)(2,1)S(1)}, u32[]{:S(2)}, u32[]{:S(2)}) collective-permute-start(bf16[64,2048]{1,0:T(8,128)(2,1)S(1)} %add_convert_fusion.1), channel_id=1, source_target_pairs={{0,8},{1,9},{2,10},{3,11},{4,12},{5,13},{6,14},{7,15},{8,0},{9,1},... | collective-permute-start | bytes 786440 | tf_op jit(solution)/shard_map/ppermute | solution.py:29
  135.2 4.5 %collective-permute-done.29 = bf16[64,2048]{1,0:T(8,128)(2,1)S(1)} collective-permute-done((bf16[64,2048]{1,0:T(8,128)(2,1)S(1)}, bf16[64,2048]{1,0:T(8,128)(2,1)S(1)}, u32[]{:S(2)}, u32[]{:S(2)}) %collective-permute-start.29) | collective-permute-done | bytes 262176 | tf_op jit(solution)/shard_map/ppermute | solution.py:29
  (89 shorter events, 14.7 us)
Async XLA Ops:
  1.6 9.0 %copy-start.1 = (bf16[64,2048]{1,0:T(8,128)(2,1)S(1)}, bf16[64,2048]{1,0:T(8,128)(2,1)}, u32[]{:S(2)}) copy-start(bf16[64,2048]{1,0:T(8,128)(2,1)} %param.11) | copy-start | bytes 786436
  4.7 2.1 %collective-permute-start = (f32[64,2048]{1,0:T(8,128)S(1)}, f32[64,2048]{1,0:T(8,128)S(1)}, u32[]{:S(2)}, u32[]{:S(2)}) collective-permute-start(f32[64,2048]{1,0:T(8,128)S(1)} %fusion.5), channel_id=1, source_target_pairs={{0,1},{1,0},{2,3},{3,2},{4,5},{5,4},{6,7},{7,6},{8,9},{9,8},{10,11... | collective-permute-start | bytes 1572872 | tf_op jit(solution)/shard_map/ppermute | solution.py:291
  6.7 7.5 %collective-permute-start.1 = (bf16[2,512,2048]{2,1,0:T(8,128)(2,1)}, bf16[2,512,2048]{2,1,0:T(8,128)(2,1)}, u32[]{:S(2)}, u32[]{:S(2)}) collective-permute-start(bf16[2,512,2048]{2,1,0:T(8,128)(2,1)} %param.15), channel_id=1, source_target_pairs={{0,1},{1,0},{2,3},{3,2},{4,5},{5,4},{6,7},{7,6},{8,9},{9,8},{10,11... | collective-permute-start | bytes 12582920 | tf_op jit(solution)/shard_map/ppermute | solution.py:56
  7.2 7.0 %copy-start.4 = (bf16[2,512,2048]{2,1,0:T(8,128)(2,1)S(1)}, bf16[2,512,2048]{2,1,0:T(8,128)(2,1)}, u32[]{:S(2)}) copy-start(bf16[2,512,2048]{2,1,0:T(8,128)(2,1)} %param.16) | copy-start | bytes 12582916
  14.2 18.4 %collective-permute-start.6 = (bf16[2,512,2048]{2,1,0:T(8,128)(2,1)S(1)}, bf16[2,512,2048]{2,1,0:T(8,128)(2,1)}, u32[]{:S(2)}, u32[]{:S(2)}) collective-permute-start(bf16[2,512,2048]{2,1,0:T(8,128)(2,1)S(1)} %copy-done.4), channel_id=1, source_target_pairs={{0,1},{1,0},{2,3},{3,2},{4,5},{5,4},{6,7},{7,6},{8,9},{9,8},{10,11... | collective-permute-start | bytes 12582920 | tf_op jit(solution)/shard_map/ppermute | solution.py:56
  14.6 12.3 %collective-permute-start.2 = (bf16[64,2176]{1,0:T(8,128)(2,1)S(1)}, bf16[64,2176]{1,0:T(8,128)(2,1)S(1)}, u32[]{:S(2)}, u32[]{:S(2)}) collective-permute-start(bf16[64,2176]{1,0:T(8,128)(2,1)S(1)} %fusion.4.refs_0_), channel_id=1, source_target_pairs={{0,24},{1,25},{2,26},{3,27},{4,28},{5,29},{6,30},{7,31},{8,16},{9,... | collective-permute-start | bytes 835592 | tf_op jit(solution)/shard_map/ppermute | solution.py:29
  19.4 13.2 %collective-permute-start.3 = (bf16[64,2176]{1,0:T(8,128)(2,1)S(1)}, bf16[64,2176]{1,0:T(8,128)(2,1)S(1)}, u32[]{:S(2)}, u32[]{:S(2)}) collective-permute-start(bf16[64,2176]{1,0:T(8,128)(2,1)S(1)} %fusion.4.refs_0_), channel_id=1, source_target_pairs={{0,8},{1,9},{2,10},{3,11},{4,12},{5,13},{6,14},{7,15},{8,0},{9,1},... | collective-permute-start | bytes 835592 | tf_op jit(solution)/shard_map/ppermute | solution.py:29
  19.4 13.2 %collective-permute-start.4 = (bf16[64,2176]{1,0:T(8,128)(2,1)S(1)}, bf16[64,2176]{1,0:T(8,128)(2,1)S(1)}, u32[]{:S(2)}, u32[]{:S(2)}) collective-permute-start(bf16[64,2176]{1,0:T(8,128)(2,1)S(1)} %fusion.4.refs_0_), channel_id=1, source_target_pairs={{0,2},{1,5},{2,0},{3,7},{4,6},{5,1},{6,4},{7,3},{8,10},{9,13},{10,... | collective-permute-start | bytes 835592 | tf_op jit(solution)/shard_map/ppermute | solution.py:29
  20.9 11.8 %collective-permute-start.5 = (bf16[64,2176]{1,0:T(8,128)(2,1)S(1)}, bf16[64,2176]{1,0:T(8,128)(2,1)S(1)}, u32[]{:S(2)}, u32[]{:S(2)}) collective-permute-start(bf16[64,2176]{1,0:T(8,128)(2,1)S(1)} %fusion.4.refs_0_), channel_id=1, source_target_pairs={{0,4},{1,3},{2,6},{3,1},{4,0},{5,7},{6,2},{7,5},{8,12},{9,11},{10,... | collective-permute-start | bytes 835592 | tf_op jit(solution)/shard_map/ppermute | solution.py:29
  33.5 13.5 %collective-permute-start.11 = (bf16[2,512,2048]{2,1,0:T(8,128)(2,1)}, bf16[2,512,2048]{2,1,0:T(8,128)(2,1)}, u32[]{:S(2)}, u32[]{:S(2)}) collective-permute-start(bf16[2,512,2048]{2,1,0:T(8,128)(2,1)} %param.17), channel_id=1, source_target_pairs={{0,1},{1,0},{2,3},{3,2},{4,5},{5,4},{6,7},{7,6},{8,9},{9,8},{10,11... | collective-permute-start | bytes 12582920 | tf_op jit(solution)/shard_map/ppermute | solution.py:56
  33.5 13.5 %collective-permute-start.9 = (bf16[96,2176]{1,0:T(8,128)(2,1)}, bf16[96,2176]{1,0:T(8,128)(2,1)S(1)}, u32[]{:S(2)}, u32[]{:S(2)}) collective-permute-start(bf16[96,2176]{1,0:T(8,128)(2,1)} %get-tuple-element.61), channel_id=1, source_target_pairs={{0,2},{1,5},{2,0},{3,7},{4,6},{5,1},{6,4},{7,3},{8,10},{9,13},{10,... | collective-permute-start | bytes 1253384 | tf_op jit(solution)/shard_map/ppermute | solution.py:29
  35.0 12.0 %collective-permute-start.10 = (bf16[96,2176]{1,0:T(8,128)(2,1)S(1)}, bf16[96,2176]{1,0:T(8,128)(2,1)S(1)}, u32[]{:S(2)}, u32[]{:S(2)}) collective-permute-start(bf16[96,2176]{1,0:T(8,128)(2,1)S(1)} %get-tuple-element.62), channel_id=1, source_target_pairs={{0,4},{1,3},{2,6},{3,1},{4,0},{5,7},{6,2},{7,5},{8,12},{9,11},{10,... | collective-permute-start | bytes 1253384 | tf_op jit(solution)/shard_map/ppermute | solution.py:29
  36.5 10.5 %collective-permute-start.7 = (bf16[64,2176]{1,0:T(8,128)(2,1)S(1)}, bf16[64,2176]{1,0:T(8,128)(2,1)}, u32[]{:S(2)}, u32[]{:S(2)}) collective-permute-start(bf16[64,2176]{1,0:T(8,128)(2,1)S(1)} %collective-permute-done.2), channel_id=1, source_target_pairs={{8,0},{9,1},{10,2},{11,3},{12,4},{13,5},{14,6},{15,7},{16,24},{17,... | collective-permute-start | bytes 835592 | tf_op jit(solution)/shard_map/ppermute | solution.py:29
  37.8 9.2 %collective-permute-start.8 = (bf16[64,2176]{1,0:T(8,128)(2,1)S(1)}, bf16[64,2176]{1,0:T(8,128)(2,1)}, u32[]{:S(2)}, u32[]{:S(2)}) collective-permute-start(bf16[64,2176]{1,0:T(8,128)(2,1)S(1)} %collective-permute-done.3.refs_3_), channel_id=1, source_target_pairs={{8,16},{9,17},{10,18},{11,19},{12,20},{13,21},{14,22},{15,23},{16,... | collective-permute-start | bytes 835592 | tf_op jit(solution)/shard_map/ppermute | solution.py:29
  48.2 17.4 %collective-permute-start.12 = (bf16[160,2176]{1,0:T(8,128)(2,1)S(1)}, bf16[160,2176]{1,0:T(8,128)(2,1)S(1)}, u32[]{:S(2)}, u32[]{:S(2)}) collective-permute-start(bf16[160,2176]{1,0:T(8,128)(2,1)S(1)} %get-tuple-element.68), channel_id=1, source_target_pairs={{0,2},{1,5},{2,0},{3,7},{4,6},{5,1},{6,4},{7,3},{8,10},{9,13},{10,... | collective-permute-start | bytes 2088968 | tf_op jit(solution)/shard_map/ppermute | solution.py:29
  48.8 16.8 %collective-permute-start.13 = (bf16[160,2176]{1,0:T(8,128)(2,1)S(1)}, bf16[160,2176]{1,0:T(8,128)(2,1)S(1)}, u32[]{:S(2)}, u32[]{:S(2)}) collective-permute-start(bf16[160,2176]{1,0:T(8,128)(2,1)S(1)} %get-tuple-element.69), channel_id=1, source_target_pairs={{0,4},{1,3},{2,6},{3,1},{4,0},{5,7},{6,2},{7,5},{8,12},{9,11},{10,... | collective-permute-start | bytes 2088968 | tf_op jit(solution)/shard_map/ppermute | solution.py:29
  65.7 9.5 %collective-permute-start.14 = (bf16[64,2176]{1,0:T(8,128)(2,1)S(1)}, bf16[64,2176]{1,0:T(8,128)(2,1)S(1)}, u32[]{:S(2)}, u32[]{:S(2)}) collective-permute-start(bf16[64,2176]{1,0:T(8,128)(2,1)S(1)} %pad_maximum_fusion.9), channel_id=1, source_target_pairs={{0,2},{1,5},{2,0},{3,7},{4,6},{5,1},{6,4},{7,3},{8,10},{9,13},{10,... | collective-permute-start | bytes 835592 | tf_op jit(solution)/shard_map/ppermute | solution.py:29
  67.2 8.1 %collective-permute-start.15 = (bf16[64,2176]{1,0:T(8,128)(2,1)S(1)}, bf16[64,2176]{1,0:T(8,128)(2,1)S(1)}, u32[]{:S(2)}, u32[]{:S(2)}) collective-permute-start(bf16[64,2176]{1,0:T(8,128)(2,1)S(1)} %pad_maximum_fusion.10), channel_id=1, source_target_pairs={{0,4},{1,3},{2,6},{3,1},{4,0},{5,7},{6,2},{7,5},{8,12},{9,11},{10,... | collective-permute-start | bytes 835592 | tf_op jit(solution)/shard_map/ppermute | solution.py:29
  90.5 8.4 %collective-permute-start.20 = (bf16[64,2048]{1,0:T(8,128)(2,1)S(1)}, bf16[64,2048]{1,0:T(8,128)(2,1)S(1)}, u32[]{:S(2)}, u32[]{:S(2)}) collective-permute-start(bf16[64,2048]{1,0:T(8,128)(2,1)S(1)} %get-tuple-element.94), channel_id=1, source_target_pairs={{0,2},{1,5},{2,0},{3,7},{4,6},{5,1},{6,4},{7,3},{8,10},{9,13},{10,... | collective-permute-start | bytes 786440 | tf_op jit(solution)/shard_map/ppermute | solution.py:29
  91.8 8.1 %collective-permute-start.16 = (bf16[64,2048]{1,0:T(8,128)(2,1)S(1)}, bf16[64,2048]{1,0:T(8,128)(2,1)S(1)}, u32[]{:S(2)}, u32[]{:S(2)}) collective-permute-start(bf16[64,2048]{1,0:T(8,128)(2,1)S(1)} %get-tuple-element.90), channel_id=1, source_target_pairs={{0,4},{1,3},{2,6},{3,1},{4,0},{5,7},{6,2},{7,5},{8,12},{9,11},{10,... | collective-permute-start | bytes 786440 | tf_op jit(solution)/shard_map/ppermute | solution.py:29
  99.0 12.1 %collective-permute-start.21 = (bf16[96,2048]{1,0:T(8,128)(2,1)S(1)}, bf16[96,2048]{1,0:T(8,128)(2,1)S(1)}, u32[]{:S(2)}, u32[]{:S(2)}) collective-permute-start(bf16[96,2048]{1,0:T(8,128)(2,1)S(1)} %pad_maximum_fusion.7), channel_id=1, source_target_pairs={{0,4},{1,3},{2,6},{3,1},{4,0},{5,7},{6,2},{7,5},{8,12},{9,11},{10,... | collective-permute-start | bytes 1179656 | tf_op jit(solution)/shard_map/ppermute | solution.py:29
  100.0 11.2 %collective-permute-start.17 = (bf16[96,2048]{1,0:T(8,128)(2,1)S(1)}, bf16[96,2048]{1,0:T(8,128)(2,1)S(1)}, u32[]{:S(2)}, u32[]{:S(2)}) collective-permute-start(bf16[96,2048]{1,0:T(8,128)(2,1)S(1)} %pad_maximum_fusion.5), channel_id=1, source_target_pairs={{0,2},{1,5},{2,0},{3,7},{4,6},{5,1},{6,4},{7,3},{8,10},{9,13},{10,... | collective-permute-start | bytes 1179656 | tf_op jit(solution)/shard_map/ppermute | solution.py:29
  102.1 16.2 %collective-permute-start.26 = (bf16[64,2048]{1,0:T(8,128)(2,1)S(1)}, bf16[64,2048]{1,0:T(8,128)(2,1)S(1)}, u32[]{:S(2)}, u32[]{:S(2)}) collective-permute-start(bf16[64,2048]{1,0:T(8,128)(2,1)S(1)} %pad_maximum_fusion.14), channel_id=1, source_target_pairs={{0,4},{1,3},{2,6},{3,1},{4,0},{5,7},{6,2},{7,5},{8,12},{9,11},{10,... | collective-permute-start | bytes 786440 | tf_op jit(solution)/shard_map/ppermute | solution.py:29
  102.5 15.8 %collective-permute-start.25 = (bf16[64,2048]{1,0:T(8,128)(2,1)S(1)}, bf16[64,2048]{1,0:T(8,128)(2,1)S(1)}, u32[]{:S(2)}, u32[]{:S(2)}) collective-permute-start(bf16[64,2048]{1,0:T(8,128)(2,1)S(1)} %pad_maximum_fusion.13), channel_id=1, source_target_pairs={{0,2},{1,5},{2,0},{3,7},{4,6},{5,1},{6,4},{7,3},{8,10},{9,13},{10,... | collective-permute-start | bytes 786440 | tf_op jit(solution)/shard_map/ppermute | solution.py:29
  111.2 8.2 %collective-permute-start.24 = (bf16[64,2048]{1,0:T(8,128)(2,1)S(1)}, bf16[64,2048]{1,0:T(8,128)(2,1)S(1)}, u32[]{:S(2)}, u32[]{:S(2)}) collective-permute-start(bf16[64,2048]{1,0:T(8,128)(2,1)S(1)} %fusion.2), channel_id=1, source_target_pairs={{0,8},{1,9},{2,10},{3,11},{4,12},{5,13},{6,14},{7,15},{24,16},{25,... | collective-permute-start | bytes 786440 | tf_op jit(solution)/shard_map/ppermute | solution.py:29
  115.6 10.9 %collective-permute-start.18 = (bf16[96,2048]{1,0:T(8,128)(2,1)S(1)}, bf16[96,2048]{1,0:T(8,128)(2,1)S(1)}, u32[]{:S(2)}, u32[]{:S(2)}) collective-permute-start(bf16[96,2048]{1,0:T(8,128)(2,1)S(1)} %pad_maximum_fusion.6), channel_id=1, source_target_pairs={{0,4},{1,3},{2,6},{3,1},{4,0},{5,7},{6,2},{7,5},{8,12},{9,11},{10,... | collective-permute-start | bytes 1179656 | tf_op jit(solution)/shard_map/ppermute | solution.py:29
  117.5 7.8 %collective-permute-start.22 = (bf16[96,2048]{1,0:T(8,128)(2,1)S(1)}, bf16[96,2048]{1,0:T(8,128)(2,1)S(1)}, u32[]{:S(2)}, u32[]{:S(2)}) collective-permute-start(bf16[96,2048]{1,0:T(8,128)(2,1)S(1)} %pad_maximum_fusion.8), channel_id=1, source_target_pairs={{0,2},{1,5},{2,0},{3,7},{4,6},{5,1},{6,4},{7,3},{8,10},{9,13},{10,... | collective-permute-start | bytes 1179656 | tf_op jit(solution)/shard_map/ppermute | solution.py:29
  119.7 7.2 %collective-permute-start.28 = (bf16[64,2048]{1,0:T(8,128)(2,1)S(1)}, bf16[64,2048]{1,0:T(8,128)(2,1)S(1)}, u32[]{:S(2)}, u32[]{:S(2)}) collective-permute-start(bf16[64,2048]{1,0:T(8,128)(2,1)S(1)} %get-tuple-element.103), channel_id=1, source_target_pairs={{8,16},{9,17},{10,18},{11,19},{12,20},{13,21},{14,22},{15,23},{16,... | collective-permute-start | bytes 786440 | tf_op jit(solution)/shard_map/ppermute | solution.py:29
  120.4 14.8 %collective-permute-start.27 = (bf16[64,2048]{1,0:T(8,128)(2,1)S(1)}, bf16[64,2048]{1,0:T(8,128)(2,1)S(1)}, u32[]{:S(2)}, u32[]{:S(2)}) collective-permute-start(bf16[64,2048]{1,0:T(8,128)(2,1)S(1)} %get-tuple-element.102), channel_id=1, source_target_pairs={{0,24},{1,25},{2,26},{3,27},{4,28},{5,29},{6,30},{7,31},{8,16},{9,... | collective-permute-start | bytes 786440 | tf_op jit(solution)/shard_map/ppermute | solution.py:29
  125.4 9.8 %collective-permute-start.23 = (bf16[64,2048]{1,0:T(8,128)(2,1)S(1)}, bf16[64,2048]{1,0:T(8,128)(2,1)S(1)}, u32[]{:S(2)}, u32[]{:S(2)}) collective-permute-start(bf16[64,2048]{1,0:T(8,128)(2,1)S(1)} %pad_maximum_fusion.12), channel_id=1, source_target_pairs={{0,4},{1,3},{2,6},{3,1},{4,0},{5,7},{6,2},{7,5},{8,12},{9,11},{10,... | collective-permute-start | bytes 786440 | tf_op jit(solution)/shard_map/ppermute | solution.py:29
  126.6 8.6 %collective-permute-start.19 = (bf16[64,2048]{1,0:T(8,128)(2,1)S(1)}, bf16[64,2048]{1,0:T(8,128)(2,1)S(1)}, u32[]{:S(2)}, u32[]{:S(2)}) collective-permute-start(bf16[64,2048]{1,0:T(8,128)(2,1)S(1)} %pad_maximum_fusion.11), channel_id=1, source_target_pairs={{0,2},{1,5},{2,0},{3,7},{4,6},{5,1},{6,4},{7,3},{8,10},{9,13},{10,... | collective-permute-start | bytes 786440 | tf_op jit(solution)/shard_map/ppermute | solution.py:29
  127.1 12.7 %collective-permute-start.29 = (bf16[64,2048]{1,0:T(8,128)(2,1)S(1)}, bf16[64,2048]{1,0:T(8,128)(2,1)S(1)}, u32[]{:S(2)}, u32[]{:S(2)}) collective-permute-start(bf16[64,2048]{1,0:T(8,128)(2,1)S(1)} %add_convert_fusion.1), channel_id=1, source_target_pairs={{0,8},{1,9},{2,10},{3,11},{4,12},{5,13},{6,14},{7,15},{8,0},{9,1},... | collective-permute-start | bytes 786440 | tf_op jit(solution)/shard_map/ppermute | solution.py:29
  (3 other events, 13.5 us)
where the time goes:
time: 141 us
  waiting for transfers between devices  50.8 us (36%)
  starting transfers between devices  44.7 us (32%)
  Pallas kernels  30.3 us (21%)
  matrix products  6.38 us (5%)
  other arithmetic  4.95 us (4%)
  local copies, waits for them, and re-layouts  2.46 us (2%)
    ppermute x26, waiting for transfers between devices, send(): return lax.ppermute(value, ('req', 'tp'), pairs)  46.6 us
    ppermute x26, starting transfers between devices, send(): return lax.ppermute(value, ('req', 'tp'), pairs)  43.4 us
    pallas_call x2, Pallas kernels, run_experts(): pl.pallas_call(functools.partial(expert_body, takes, gives, tile, group),...  30.3 us
    dot_general x1, matrix products, project(): kept = jnp.dot(ours, out_weight, preferred_element_type=jnp.float32)  3.18 us
    dot_general x1, matrix products, project(): sent = jnp.dot(theirs, out_weight, preferred_element_type=jnp.float32)  3.07 us
  transfers between devices with their start and end apart: 30, of which 12 were waited for; matrix products, arithmetic and copies ran while one was open for 5% of the time, Pallas kernels for 11%

commit v1 on v0

--- a/solution.py
+++ b/solution.py
@@ -58,10 +58,10 @@
     gate_w, up_w, down_w = weights
     swap(gate_w)
     own, up_w, swapped[0] = together(own, up_w, swapped[0])
+    y0 = send(own, ACROSS_Y)
+    x0 = send(own, ACROSS_X)
+    pair = send(own, PAIR_Z)
     over = send(own, OPPOSITE_Z)
-    pair = send(own, PAIR_Z)
-    x0 = send(own, ACROSS_X)
-    y0 = send(own, ACROSS_Y)
     swap(up_w)
     over, pair, x0, y0, swapped[1] = together(over, pair, x0, y0, swapped[1])
     to_x = joined(pair, y0[:half])
@@ -105,39 +105,42 @@
             value[:half], narrow(wide(value[half:rows]) + wide(term)), value[rows:]
         )
 
+    z = lax.axis_index("req") // 4
+    middle = (z == 1) | (z == 2)
     by_x = send(x3, ACROSS_X)
     by_y = send(y3, ACROSS_Y)
     x_sum = send(high(x_far2, by_y[half:]), ACROSS_X)
     y_sum = send(low(y_far2, by_x[half:]), ACROSS_Y)
-    z = lax.axis_index("req") // 4
-    middle = (z == 1) | (z == 2)
-    far2 = wide(far2) + wide(x_sum) + wide(y_sum)
-    next_ = send(narrow(far2), MIDDLE_Z)
-    x_sum = send(high(x_far1, by_y[:half]), ACROSS_X)
-    y_sum = send(low(y_far1, by_x[:half]), ACROSS_Y)
+    x_far1, y_far1 = high(x_far1, by_y[:half]), low(y_far1, by_x[:half])
+    x_far1, y_far1, x_sum, y_sum = together(x_far1, y_far1, x_sum, y_sum)
+    next_ = send(narrow(wide(far2) + wide(x_sum) + wide(y_sum)), OPPOSITE_Z)
+    x_sum = send(x_far1, ACROSS_X)
+    y_sum = send(y_far1, ACROSS_Y)
     far1 = wide(far1) + wide(x_sum[:rows]) + wide(y_sum[:rows])
     inward = send(narrow(far1), INWARD_Z)
-    over = send(narrow(jnp.where(middle, far1 + wide(inward), far2)), OPPOSITE_Z)
+    near = send(narrow(far1 + wide(inward)), MIDDLE_Z)
     x_pair = send(high(x1, y_sum[rows:]), ACROSS_X)
     y_pair = send(low(y1, x_sum[rows:]), ACROSS_Y)
     pair = wide(pair) + wide(x_pair[:rows]) + wide(y_pair[:rows])
-    by_pair = send(narrow(pair + wide(next_)), PAIR_Z)
+    pair = narrow(pair + jnp.where(middle, wide(next_), 0.0))
+    by_pair = send(pair, PAIR_Z)
     x_own = send(high(x0, y_pair[rows:]), ACROSS_X)
     y_own = send(low(y0, x_pair[rows:]), ACROSS_Y)
-    total = wide(own) + wide(x_own) + wide(y_own)
-    return total + wide(over) + wide(by_pair)
-
-
-def expert_body(takes, gives, tile, group, *refs):
+    total = wide(own) + wide(x_own) + wide(y_own) + jnp.where(middle, 0.0, wide(next_))
+    return total + wide(near) + wide(by_pair)
+
+
+def expert_body(takes, gives, tile, group, loads, *refs):
     pieces = len({i for i, _, _ in takes})
-    blocks = refs[:pieces]
-    router, local, gate_own, up_own, down_own, gate_far, up_far, down_far = refs[
-        pieces : pieces + 8
-    ]
-    outs = refs[pieces + 8 : pieces + 8 + len(gives)]
-    held, picks, spreads, sel, acts, ups, downs, up_sem, down_sem = refs[
-        pieces + 8 + len(gives) :
-    ]
+    blocks, refs = refs[:pieces], refs[pieces:]
+    if loads:
+        router, local, gate_own, up_own, down_own, gate_far, up_far, down_far = refs[:8]
+        outs, (ups, downs) = refs[8 : 8 + len(gives)], refs[8 + len(gives) :][:2]
+        held, picks, spreads, sel, acts, up_sem, down_sem = refs[10 + len(gives) :]
+    else:
+        router, local, ups, downs = refs[:4]
+        outs = refs[4 : 4 + len(gives)]
+        held, picks, spreads, sel, acts = refs[4 + len(gives) :]
     total_rows, width = held.shape
     experts = router.shape[1]
     tiles = acts.shape[1]
@@ -145,7 +148,7 @@
     slots = group // 2
 
     def up_copies(t):
-        part = pl.ds(pl.multiple_of(t * tile, tile), tile)
+        part = pl.ds(t * tile, tile)
         return [
             pltpu.make_async_copy(w.at[part, :], ups.at[i, t], up_sem.at[i, t])
             for i, w in enumerate((gate_own, up_own, gate_far, up_far))
@@ -156,9 +159,12 @@
             (down_own, down_far)[i], downs.at[i], down_sem.at[i]
         )
 
-    for t in range(min(2, tiles)):
-        for copy in up_copies(t):
-            copy.start()
+    if loads:
+        for t in range(tiles):
+            for copy in up_copies(t):
+                copy.start()
+        for i in range(2):
+            down_copy(i).start()
     at = 0
     for i, start, size in takes:
         held[at : at + size, :] = blocks[i][start : start + size, :width]
@@ -190,19 +196,10 @@
         for j in range(2):
             sel[j, g * slots : (g + 1) * slots, :] = rows[j * slots : (j + 1) * slots, :]
 
-    def up(t, _):
-        @pl.when(t + 2 < tiles)
-        def _():
-            for copy in up_copies(t + 2):
-                copy.start()
-
-        @pl.when(t + 2 == tiles)
-        def _():
-            for i in range(2):
-                down_copy(i).start()
-
-        for copy in up_copies(t):
-            copy.wait()
+    for t in range(tiles):
+        if loads:
+            for copy in up_copies(t):
+                copy.wait()
         x = sel[t // (tiles // 2)]
         for i in range(2):
             h = lax.dot_general(x, ups[2 * i, t], NT, preferred_element_type=jnp.float32)
@@ -210,11 +207,9 @@
                 x, ups[2 * i + 1, t], NT, preferred_element_type=jnp.float32
             )
             acts[i, t] = (h / (1.0 + jnp.exp(-h)) * u).astype(jnp.bfloat16)
-        return 0
-
-    lax.fori_loop(0, tiles, up, 0)
-    for i in range(2):
-        down_copy(i).wait()
+    if loads:
+        for i in range(2):
+            down_copy(i).wait()
 
     def down(n, _):
         part = pl.ds(pl.multiple_of(n * tile, tile), tile)
@@ -248,38 +243,49 @@
                 at += size
         return 0
 
-    lax.fori_loop(0, width // tile, down, 0)
-
-
-def run_experts(blocks, takes, gives, router, local, own, far, tile=256, group=256):
+    lax.fori_loop(0, width // tile, down, 0, unroll=True)
+
+
+def run_experts(blocks, takes, gives, router, local, weights, loads, tile=256, group=256):
     width = router.shape[0]
-    hidden = own[0].shape[0]
+    if loads:
+        hidden = weights[0].shape[0]
+        tiles = hidden // tile
+        copies = [
+            pltpu.VMEM((4, tiles, tile, width), jnp.bfloat16),
+            pltpu.VMEM((2, hidden, width), jnp.bfloat16),
+        ]
+    else:
+        hidden = weights[1].shape[1]
+        tiles = hidden // tile
+        copies = []
+        weights = [pltpu.with_memory_space_constraint(w, pltpu.VMEM) for w in weights]
     total_rows = sum(size for _, _, size in takes)
     sizes = [sum(size for _, size in ranges) for ranges in gives]
     vmem = pl.BlockSpec(memory_space=pltpu.VMEM)
+    held_out = pl.BlockSpec(memory_space=pl.ANY)
+    semaphores = [pltpu.SemaphoreType.DMA((4, tiles)), pltpu.SemaphoreType.DMA((2,))]
     return pl.pallas_call(
-        functools.partial(expert_body, takes, gives, tile, group),
-        in_specs=[vmem] * (len(blocks) + 2) + [pl.BlockSpec(memory_space=pl.ANY)] * 6,
-        out_specs=[vmem] * len(sizes),
-        out_shape=[jax.ShapeDtypeStruct((size, width), jnp.bfloat16) for size in sizes],
+        functools.partial(expert_body, takes, gives, tile, group, loads),
+        in_specs=[vmem] * (len(blocks) + 2) + [held_out if loads else vmem] * len(weights),
+        out_specs=[vmem] * (len(sizes) + len(copies)),
+        out_shape=[jax.ShapeDtypeStruct((size, width), jnp.bfloat16) for size in sizes]
+        + copies,
         scratch_shapes=[
             pltpu.VMEM((total_rows, width), jnp.bfloat16),
             pltpu.VMEM((total_rows, 128), jnp.bfloat16),
             pltpu.VMEM((total_rows // group, group, group), jnp.bfloat16),
             pltpu.VMEM((2, total_rows // 2, width), jnp.bfloat16),
-            pltpu.VMEM((2, hidden // tile, total_rows // 2, tile), jnp.bfloat16),
-            pltpu.VMEM((4, hidden // tile, tile, width), jnp.bfloat16),
-            pltpu.VMEM((2, hidden, width), jnp.bfloat16),
-            pltpu.SemaphoreType.DMA((4, hidden // tile)),
-            pltpu.SemaphoreType.DMA((2,)),
-        ],
-        compiler_params=pltpu.CompilerParams(vmem_limit_bytes=42 * 1024 * 1024),
+            pltpu.VMEM((2, tiles, total_rows // 2, tile), jnp.bfloat16),
+        ]
+        + (semaphores if loads else []),
+        compiler_params=pltpu.CompilerParams(vmem_limit_bytes=24 * 1024 * 1024),
         cost_estimate=pl.CostEstimate(
             flops=8 * total_rows * width * hidden,
             bytes_accessed=12 * hidden * width + 4 * total_rows * width,
             transcendentals=total_rows * hidden,
         ),
-    )(*blocks, router, local, *own, *far)
+    )(*blocks, router, local, *weights)
 
 
 def project(attn, out_weight, stream_in, later):
@@ -319,13 +325,13 @@
     own = tuple(w.reshape(-1, width) for w in weights)
     first, far1, far2, x2, y2, far = spread(jnp.concatenate([normed, slot], axis=1), weights)
     far = tuple(w.reshape(-1, width) for w in far)
-    run = functools.partial(run_experts, router=router_weight, local=local, own=own, far=far)
+    run = functools.partial(run_experts, router=router_weight, local=local)
     takes = tuple((i, 0, rows) for i in range(7)) + ((4, rows, half), (5, rows, half))
     gives = tuple(((i * rows, rows),) for i in range(4))
     gives += (((4 * rows, rows), (7 * rows, half)),)
     gives += (((5 * rows, rows), (7 * rows + half, half)),)
     gives += (((6 * rows, rows),),)
-    done = run(first + [far1], takes, gives)
+    *done, ups, downs = run(first + [far1], takes, gives, weights=(*own, *far), loads=True)
     x2, y2, *done = lax.optimization_barrier((x2, y2, *done))
     x3, y3 = spread_last(x2, y2, rows)
     first, (far1,) = done[:6], done[6:]
@@ -340,7 +346,9 @@
         ((5 * rows + half, half), (6 * rows + half, half)),
         ((7 * rows, rows),),
     )
-    *second, far2 = run([x2, y2, x3, y3, far2], takes, gives)
+    *second, far2 = run(
+        [x2, y2, x3, y3, far2], takes, gives, weights=(ups, downs), loads=False
+    )
     second = [far1, far2, *second]
     mix = collect(first, second)
     return (hidden_state.astype(jnp.bfloat16), mix.astype(jnp.bfloat16))

time: 141 us -> 139 us (0.986)
  waiting for transfers between devices: 50.8 us -> 62.4 us
  Pallas kernels: 30.3 us -> 23.1 us
  starting transfers between devices: 44.7 us -> 38 us
    ppermute x26, waiting for transfers between devices: 46.6 us -> 58.2 us  [send(): return lax.ppermute(value, ('req', 'tp'), pairs)]
    pallas_call x2, Pallas kernels: 30.3 us -> 23.1 us  [run_experts(): pl.pallas_call(functools.partial(expert_body, takes, gives, tile, group,...]
    ppermute x26, starting transfers between devices: 43.4 us -> 36.8 us  [send(): return lax.ppermute(value, ('req', 'tp'), pairs)]
  transfers between devices with their start and end apart: 30 -> 30, of which waited for: 12 -> 18; matrix products, arithmetic and copies ran while one was open for 5% -> 5% of each run, Pallas kernels for 11% -> 10%
where the time goes in v1:
time: 139 us; the launch traced here: 138 us
  waiting for transfers between devices  62.4 us (45%)
  starting transfers between devices  38 us (27%)
  Pallas kernels  23.1 us (17%)
  matrix products  6.38 us (5%)
  other arithmetic  4.96 us (4%)
  local copies, waits for them, and re-layouts  2.47 us (2%)
    ppermute x26, waiting for transfers between devices, send(): return lax.ppermute(value, ('req', 'tp'), pairs)  58.2 us
    ppermute x26, starting transfers between devices, send(): return lax.ppermute(value, ('req', 'tp'), pairs)  36.8 us
    pallas_call x2, Pallas kernels, run_experts(): pl.pallas_call(functools.partial(expert_body, takes, gives, tile, group,...  23.1 us
    dot_general x1, matrix products, project(): kept = jnp.dot(ours, out_weight, preferred_element_type=jnp.float32)  3.18 us
    dot_general x1, matrix products, project(): sent = jnp.dot(theirs, out_weight, preferred_element_type=jnp.float32)  3.07 us
  transfers between devices with their start and end apart: 30, of which 18 were waited for; matrix products, arithmetic and copies ran while one was open for 5% of the time, Pallas kernels for 10%

profile of v1, /device:TPU:0, one launch (start us, length us, event | category | flops | bytes accessed | tf_op | source)
XLA Modules:
  0.0 138.3 jit_solution(13870079159355664989)
XLA Ops:
  1.6 3.1 %fusion.10 = f32[64,2048]{1,0:T(8,128)S(1)} fusion(bf16[1024,2048]{1,0:T(8,128)(2,1)} %param.10, bf16[128,1024]{1,0:T(8,128)(2,1)S(1)} %copy-done, s32[]{:T(128)S(6)} %select_n.39), kind=kOutput, calls=%fused_computation.46 | convolution fusion | flops 268435456 | bytes 4849668 | tf_op jit(solution)/shard_map/dot_general | solution.py:296
  5.2 1.5 %collective-permute-done = f32[64,2048]{1,0:T(8,128)S(1)} collective-permute-done((f32[64,2048]{1,0:T(8,128)S(1)}, f32[64,2048]{1,0:T(8,128)S(1)}, u32[]{:S(2)}, u32[]{:S(2)}) %collective-permute-start) | collective-permute-done | bytes 524320 | tf_op jit(solution)/shard_map/ppermute | solution.py:297
  7.4 3.2 %fusion.12 = f32[64,2048]{1,0:T(8,128)S(1)} fusion(bf16[1024,2048]{1,0:T(8,128)(2,1)} %param.10, bf16[128,1024]{1,0:T(8,128)(2,1)S(1)} %copy-done, s32[]{:T(128)S(6)} %select_n.38), kind=kOutput, calls=%fused_computation.48 | convolution fusion | flops 268435456 | bytes 4849668 | tf_op jit(solution)/shard_map/dot_general | solution.py:298
  11.6 2.7 %collective-permute-done.1 = bf16[2,512,2048]{2,1,0:T(8,128)(2,1)} collective-permute-done((bf16[2,512,2048]{2,1,0:T(8,128)(2,1)}, bf16[2,512,2048]{2,1,0:T(8,128)(2,1)}, u32[]{:S(2)}, u32[]{:S(2)}) %collective-permute-start.1) | collective-permute-done | bytes 4194336 | tf_op jit(solution)/shard_map/ppermute | solution.py:56
  14.6 2.7 %collective-permute-start.5 = (bf16[64,2176]{1,0:T(8,128)(2,1)S(1)}, bf16[64,2176]{1,0:T(8,128)(2,1)S(1)}, u32[]{:S(2)}, u32[]{:S(2)}) collective-permute-start(bf16[64,2176]{1,0:T(8,128)(2,1)S(1)} %fusion.9.refs_0_), channel_id=1, source_target_pairs={{0,4},{1,3},{2,6},{3,1},{4,0},{5,7},{6,2},{7,5},{8,12},{9,11},{10,... | collective-permute-start | bytes 835592 | tf_op jit(solution)/shard_map/ppermute | solution.py:29
  17.3 1.5 %collective-permute-start.4 = (bf16[64,2176]{1,0:T(8,128)(2,1)S(1)}, bf16[64,2176]{1,0:T(8,128)(2,1)S(1)}, u32[]{:S(2)}, u32[]{:S(2)}) collective-permute-start(bf16[64,2176]{1,0:T(8,128)(2,1)S(1)} %fusion.9.refs_0_), channel_id=1, source_target_pairs={{0,2},{1,5},{2,0},{3,7},{4,6},{5,1},{6,4},{7,3},{8,10},{9,13},{10,... | collective-permute-start | bytes 835592 | tf_op jit(solution)/shard_map/ppermute | solution.py:29
  18.8 1.6 %collective-permute-start.3 = (bf16[64,2176]{1,0:T(8,128)(2,1)S(1)}, bf16[64,2176]{1,0:T(8,128)(2,1)S(1)}, u32[]{:S(2)}, u32[]{:S(2)}) collective-permute-start(bf16[64,2176]{1,0:T(8,128)(2,1)S(1)} %fusion.9.refs_0_), channel_id=1, source_target_pairs={{0,8},{1,9},{2,10},{3,11},{4,12},{5,13},{6,14},{7,15},{8,0},{9,1},... | collective-permute-start | bytes 835592 | tf_op jit(solution)/shard_map/ppermute | solution.py:29
  20.3 2.5 %collective-permute-start.2 = (bf16[64,2176]{1,0:T(8,128)(2,1)S(1)}, bf16[64,2176]{1,0:T(8,128)(2,1)S(1)}, u32[]{:S(2)}, u32[]{:S(2)}) collective-permute-start(bf16[64,2176]{1,0:T(8,128)(2,1)S(1)} %fusion.9.refs_0_), channel_id=1, source_target_pairs={{0,24},{1,25},{2,26},{3,27},{4,28},{5,29},{6,30},{7,31},{8,16},{9,... | collective-permute-start | bytes 835592 | tf_op jit(solution)/shard_map/ppermute | solution.py:29
  24.4 3.0 %collective-permute-done.3.refs_3_ = bf16[64,2176]{1,0:T(8,128)(2,1)S(1)} collective-permute-done((bf16[64,2176]{1,0:T(8,128)(2,1)S(1)}, bf16[64,2176]{1,0:T(8,128)(2,1)S(1)}, u32[]{:S(2)}, u32[]{:S(2)}) %collective-permute-start.3) | collective-permute-done | bytes 278560 | tf_op jit(solution)/shard_map/ppermute | solution.py:29
  27.4 7.8 %collective-permute-done.2 = bf16[64,2176]{1,0:T(8,128)(2,1)S(1)} collective-permute-done((bf16[64,2176]{1,0:T(8,128)(2,1)S(1)}, bf16[64,2176]{1,0:T(8,128)(2,1)S(1)}, u32[]{:S(2)}, u32[]{:S(2)}) %collective-permute-start.2) | collective-permute-done | bytes 278560 | tf_op jit(solution)/shard_map/ppermute | solution.py:29
  37.2 1.3 collective-permute-start.7
  38.4 1.4 collective-permute-start.8
  41.1 6.6 %collective-permute-done.7 = bf16[64,2176]{1,0:T(8,128)(2,1)} collective-permute-done((bf16[64,2176]{1,0:T(8,128)(2,1)S(1)}, bf16[64,2176]{1,0:T(8,128)(2,1)}, u32[]{:S(2)}, u32[]{:S(2)}) %collective-permute-start.7) | collective-permute-done | bytes 278560 | tf_op jit(solution)/shard_map/ppermute | solution.py:29
  50.4 1.5 %collective-permute-start.13 = (bf16[160,2176]{1,0:T(8,128)(2,1)S(1)}, bf16[160,2176]{1,0:T(8,128)(2,1)S(1)}, u32[]{:S(2)}, u32[]{:S(2)}) collective-permute-start(bf16[160,2176]{1,0:T(8,128)(2,1)S(1)} %get-tuple-element.75), channel_id=1, source_target_pairs={{0,4},{1,3},{2,6},{3,1},{4,0},{5,7},{6,2},{7,5},{8,12},{9,11},{10,... | collective-permute-start | bytes 2088968 | tf_op jit(solution)/shard_map/ppermute | solution.py:29
  51.9 13.3 %shard_map.104 = (bf16[64,2048]{1,0:T(8,128)(2,1)S(1)}, bf16[64,2048]{1,0:T(8,128)(2,1)S(1)}, bf16[64,2048]{1,0:T(8,128)(2,1)S(1)}, bf16[64,2048]{1,0:T(8,128)(2...) custom-call(bf16[64,2176]{1,0:T(8,128)(2,1)S(1)} %fusion.9.refs_0_, ...), custom_call_target="tpu_custom_call" | custom-call | flops 8589934592 | bytes 29360128 | tf_op jit(solution)/shard_map/pallas_call | solution.py:268
  65.2 2.5 %collective-permute-done.12.refs_0_ = bf16[160,2176]{1,0:T(8,128)(2,1)S(1)} collective-permute-done((bf16[160,2176]{1,0:T(8,128)(2,1)S(1)}, bf16[160,2176]{1,0:T(8,128)(2,1)S(1)}, u32[]{:S(2)}, u32[]{:S(2)}) %collective-permute-start.12) | collective-permute-done | bytes 696352 | tf_op jit(solution)/shard_map/ppermute | solution.py:29
  69.6 7.5 %collective-permute-done.14.refs_2_ = bf16[64,2176]{1,0:T(8,128)(2,1)S(1)} collective-permute-done((bf16[64,2176]{1,0:T(8,128)(2,1)S(1)}, bf16[64,2176]{1,0:T(8,128)(2,1)S(1)}, u32[]{:S(2)}, u32[]{:S(2)}) %collective-permute-start.14) | collective-permute-done | bytes 278560 | tf_op jit(solution)/shard_map/ppermute | solution.py:29
  77.0 9.8 %shard_map.105 = (bf16[96,2048]{1,0:T(8,128)(2,1)S(1)}, bf16[64,2048]{1,0:T(8,128)(2,1)S(1)}, bf16[96,2048]{1,0:T(8,128)(2,1)S(1)}, bf16[64,2048]{1,0:T(8,128)(2...) custom-call(bf16[160,2176]{1,0:T(8,128)(2,1)S(1)} %collective-permute-done.12.refs, ...), custom_call_target="tpu_custom_call" | custom-call | flops 8589934592 | bytes 29360128 | tf_op jit(solution)/shard_map/pallas_call | solution.py:268
  88.9 6.1 %collective-permute-done.16 = bf16[64,2048]{1,0:T(8,128)(2,1)S(1)} collective-permute-done((bf16[64,2048]{1,0:T(8,128)(2,1)S(1)}, bf16[64,2048]{1,0:T(8,128)(2,1)S(1)}, u32[]{:S(2)}, u32[]{:S(2)}) %collective-permute-start.16) | collective-permute-done | bytes 262176 | tf_op jit(solution)/shard_map/ppermute | solution.py:29
  96.5 1.8 %collective-permute-start.19 = (bf16[64,2048]{1,0:T(8,128)(2,1)S(1)}, bf16[64,2048]{1,0:T(8,128)(2,1)S(1)}, u32[]{:S(2)}, u32[]{:S(2)}) collective-permute-start(bf16[64,2048]{1,0:T(8,128)(2,1)S(1)} %pad_maximum_fusion.12), channel_id=1, source_target_pairs={{0,4},{1,3},{2,6},{3,1},{4,0},{5,7},{6,2},{7,5},{8,12},{9,11},{10,... | collective-permute-start | bytes 786440 | tf_op jit(solution)/shard_map/ppermute | solution.py:29
  98.3 4.6 %collective-permute-done.18 = bf16[64,2048]{1,0:T(8,128)(2,1)S(1)} collective-permute-done((bf16[64,2048]{1,0:T(8,128)(2,1)S(1)}, bf16[64,2048]{1,0:T(8,128)(2,1)S(1)}, u32[]{:S(2)}, u32[]{:S(2)}) %collective-permute-start.18) | collective-permute-done | bytes 262176 | tf_op jit(solution)/shard_map/ppermute | solution.py:29
  103.0 1.7 %collective-permute-start.20 = (bf16[96,2048]{1,0:T(8,128)(2,1)S(1)}, bf16[96,2048]{1,0:T(8,128)(2,1)S(1)}, u32[]{:S(2)}, u32[]{:S(2)}) collective-permute-start(bf16[96,2048]{1,0:T(8,128)(2,1)S(1)} %pad_maximum_fusion.5), channel_id=1, source_target_pairs={{0,2},{1,5},{2,0},{3,7},{4,6},{5,1},{6,4},{7,3},{8,10},{9,13},{10,... | collective-permute-start | bytes 1179656 | tf_op jit(solution)/shard_map/ppermute | solution.py:29
  104.8 1.5 %collective-permute-start.26 = (bf16[64,2048]{1,0:T(8,128)(2,1)S(1)}, bf16[64,2048]{1,0:T(8,128)(2,1)S(1)}, u32[]{:S(2)}, u32[]{:S(2)}) collective-permute-start(bf16[64,2048]{1,0:T(8,128)(2,1)S(1)} %add_convert_fusion.1), channel_id=1, source_target_pairs={{0,24},{1,25},{2,26},{3,27},{4,28},{5,29},{6,30},{7,31},{8,16},{9,... | collective-permute-start | bytes 786440 | tf_op jit(solution)/shard_map/ppermute | solution.py:29
  106.3 1.6 %collective-permute-start.23 = (bf16[96,2048]{1,0:T(8,128)(2,1)S(1)}, bf16[96,2048]{1,0:T(8,128)(2,1)S(1)}, u32[]{:S(2)}, u32[]{:S(2)}) collective-permute-start(bf16[96,2048]{1,0:T(8,128)(2,1)S(1)} %pad_maximum_fusion.6), channel_id=1, source_target_pairs={{0,4},{1,3},{2,6},{3,1},{4,0},{5,7},{6,2},{7,5},{8,12},{9,11},{10,... | collective-permute-start | bytes 1179656 | tf_op jit(solution)/shard_map/ppermute | solution.py:29
  107.9 6.3 %collective-permute-done.20 = bf16[96,2048]{1,0:T(8,128)(2,1)S(1)} collective-permute-done((bf16[96,2048]{1,0:T(8,128)(2,1)S(1)}, bf16[96,2048]{1,0:T(8,128)(2,1)S(1)}, u32[]{:S(2)}, u32[]{:S(2)}) %collective-permute-start.20) | collective-permute-done | bytes 393248 | tf_op jit(solution)/shard_map/ppermute | solution.py:29
  114.3 2.7 %collective-permute-start.21 = (bf16[96,2048]{1,0:T(8,128)(2,1)S(1)}, bf16[96,2048]{1,0:T(8,128)(2,1)S(1)}, u32[]{:S(2)}, u32[]{:S(2)}) collective-permute-start(bf16[96,2048]{1,0:T(8,128)(2,1)S(1)} %pad_maximum_fusion.7), channel_id=1, source_target_pairs={{0,4},{1,3},{2,6},{3,1},{4,0},{5,7},{6,2},{7,5},{8,12},{9,11},{10,... | collective-permute-start | bytes 1179656 | tf_op jit(solution)/shard_map/ppermute | solution.py:29
  117.0 4.3 %collective-permute-start.27 = (bf16[64,2048]{1,0:T(8,128)(2,1)S(1)}, bf16[64,2048]{1,0:T(8,128)(2,1)S(1)}, u32[]{:S(2)}, u32[]{:S(2)}) collective-permute-start(bf16[64,2048]{1,0:T(8,128)(2,1)S(1)} %fusion.8), channel_id=1, source_target_pairs={{0,8},{1,9},{2,10},{3,11},{4,12},{5,13},{6,14},{7,15},{24,16},{25,... | collective-permute-start | bytes 786440 | tf_op jit(solution)/shard_map/ppermute | solution.py:29
  121.8 4.1 %collective-permute-done.27 = bf16[64,2048]{1,0:T(8,128)(2,1)S(1)} collective-permute-done((bf16[64,2048]{1,0:T(8,128)(2,1)S(1)}, bf16[64,2048]{1,0:T(8,128)(2,1)S(1)}, u32[]{:S(2)}, u32[]{:S(2)}) %collective-permute-start.27) | collective-permute-done | bytes 262176 | tf_op jit(solution)/shard_map/ppermute | solution.py:29
  127.1 2.2 %collective-permute-done.24 = bf16[96,2048]{1,0:T(8,128)(2,1)S(1)} collective-permute-done((bf16[96,2048]{1,0:T(8,128)(2,1)S(1)}, bf16[96,2048]{1,0:T(8,128)(2,1)S(1)}, u32[]{:S(2)}, u32[]{:S(2)}) %collective-permute-start.24) | collective-permute-done | bytes 393248 | tf_op jit(solution)/shard_map/ppermute | solution.py:29
  130.3 1.9 %collective-permute-start.29 = (bf16[64,2048]{1,0:T(8,128)(2,1)S(1)}, bf16[64,2048]{1,0:T(8,128)(2,1)S(1)}, u32[]{:S(2)}, u32[]{:S(2)}) collective-permute-start(bf16[64,2048]{1,0:T(8,128)(2,1)S(1)} %fusion.7), channel_id=1, source_target_pairs={{0,8},{1,9},{2,10},{3,11},{4,12},{5,13},{6,14},{7,15},{8,0},{9,1},... | collective-permute-start | bytes 786440 | tf_op jit(solution)/shard_map/ppermute | solution.py:29
  132.2 3.1 %collective-permute-done.22 = bf16[64,2048]{1,0:T(8,128)(2,1)S(1)} collective-permute-done((bf16[64,2048]{1,0:T(8,128)(2,1)S(1)}, bf16[64,2048]{1,0:T(8,128)(2,1)S(1)}, u32[]{:S(2)}, u32[]{:S(2)}) %collective-permute-start.22) | collective-permute-done | bytes 262176 | tf_op jit(solution)/shard_map/ppermute | solution.py:29
  135.8 1.6 %collective-permute-done.29 = bf16[64,2048]{1,0:T(8,128)(2,1)S(1)} collective-permute-done((bf16[64,2048]{1,0:T(8,128)(2,1)S(1)}, bf16[64,2048]{1,0:T(8,128)(2,1)S(1)}, u32[]{:S(2)}, u32[]{:S(2)}) %collective-permute-start.29) | collective-permute-done | bytes 262176 | tf_op jit(solution)/shard_map/ppermute | solution.py:29
  (92 shorter events, 20.5 us)
Async XLA Ops:
  1.6 9.0 %copy-start.2 = (bf16[64,2048]{1,0:T(8,128)(2,1)S(1)}, bf16[64,2048]{1,0:T(8,128)(2,1)}, u32[]{:S(2)}) copy-start(bf16[64,2048]{1,0:T(8,128)(2,1)} %param.11) | copy-start | bytes 786436
  4.7 2.1 %collective-permute-start = (f32[64,2048]{1,0:T(8,128)S(1)}, f32[64,2048]{1,0:T(8,128)S(1)}, u32[]{:S(2)}, u32[]{:S(2)}) collective-permute-start(f32[64,2048]{1,0:T(8,128)S(1)} %fusion.10), channel_id=1, source_target_pairs={{0,1},{1,0},{2,3},{3,2},{4,5},{5,4},{6,7},{7,6},{8,9},{9,8},{10,11... | collective-permute-start | bytes 1572872 | tf_op jit(solution)/shard_map/ppermute | solution.py:297
  6.7 7.5 %collective-permute-start.1 = (bf16[2,512,2048]{2,1,0:T(8,128)(2,1)}, bf16[2,512,2048]{2,1,0:T(8,128)(2,1)}, u32[]{:S(2)}, u32[]{:S(2)}) collective-permute-start(bf16[2,512,2048]{2,1,0:T(8,128)(2,1)} %param.15), channel_id=1, source_target_pairs={{0,1},{1,0},{2,3},{3,2},{4,5},{5,4},{6,7},{7,6},{8,9},{9,8},{10,11... | collective-permute-start | bytes 12582920 | tf_op jit(solution)/shard_map/ppermute | solution.py:56
  14.2 21.0 %collective-permute-start.6 = (bf16[2,512,2048]{2,1,0:T(8,128)(2,1)S(1)}, bf16[2,512,2048]{2,1,0:T(8,128)(2,1)}, u32[]{:S(2)}, u32[]{:S(2)}) collective-permute-start(bf16[2,512,2048]{2,1,0:T(8,128)(2,1)S(1)} %copy-done.5), channel_id=1, source_target_pairs={{0,1},{1,0},{2,3},{3,2},{4,5},{5,4},{6,7},{7,6},{8,9},{9,8},{10,11... | collective-permute-start | bytes 12582920 | tf_op jit(solution)/shard_map/ppermute | solution.py:56
  14.6 9.1 %collective-permute-start.5 = (bf16[64,2176]{1,0:T(8,128)(2,1)S(1)}, bf16[64,2176]{1,0:T(8,128)(2,1)S(1)}, u32[]{:S(2)}, u32[]{:S(2)}) collective-permute-start(bf16[64,2176]{1,0:T(8,128)(2,1)S(1)} %fusion.9.refs_0_), channel_id=1, source_target_pairs={{0,4},{1,3},{2,6},{3,1},{4,0},{5,7},{6,2},{7,5},{8,12},{9,11},{10,... | collective-permute-start | bytes 835592 | tf_op jit(solution)/shard_map/ppermute | solution.py:29
  17.3 7.2 %collective-permute-start.4 = (bf16[64,2176]{1,0:T(8,128)(2,1)S(1)}, bf16[64,2176]{1,0:T(8,128)(2,1)S(1)}, u32[]{:S(2)}, u32[]{:S(2)}) collective-permute-start(bf16[64,2176]{1,0:T(8,128)(2,1)S(1)} %fusion.9.refs_0_), channel_id=1, source_target_pairs={{0,2},{1,5},{2,0},{3,7},{4,6},{5,1},{6,4},{7,3},{8,10},{9,13},{10,... | collective-permute-start | bytes 835592 | tf_op jit(solution)/shard_map/ppermute | solution.py:29
  18.8 8.6 %collective-permute-start.3 = (bf16[64,2176]{1,0:T(8,128)(2,1)S(1)}, bf16[64,2176]{1,0:T(8,128)(2,1)S(1)}, u32[]{:S(2)}, u32[]{:S(2)}) collective-permute-start(bf16[64,2176]{1,0:T(8,128)(2,1)S(1)} %fusion.9.refs_0_), channel_id=1, source_target_pairs={{0,8},{1,9},{2,10},{3,11},{4,12},{5,13},{6,14},{7,15},{8,0},{9,1},... | collective-permute-start | bytes 835592 | tf_op jit(solution)/shard_map/ppermute | solution.py:29
  20.3 14.9 %collective-permute-start.2 = (bf16[64,2176]{1,0:T(8,128)(2,1)S(1)}, bf16[64,2176]{1,0:T(8,128)(2,1)S(1)}, u32[]{:S(2)}, u32[]{:S(2)}) collective-permute-start(bf16[64,2176]{1,0:T(8,128)(2,1)S(1)} %fusion.9.refs_0_), channel_id=1, source_target_pairs={{0,24},{1,25},{2,26},{3,27},{4,28},{5,29},{6,30},{7,31},{8,16},{9,... | collective-permute-start | bytes 835592 | tf_op jit(solution)/shard_map/ppermute | solution.py:29
  36.1 12.3 %collective-permute-start.11 = (bf16[2,512,2048]{2,1,0:T(8,128)(2,1)}, bf16[2,512,2048]{2,1,0:T(8,128)(2,1)}, u32[]{:S(2)}, u32[]{:S(2)}) collective-permute-start(bf16[2,512,2048]{2,1,0:T(8,128)(2,1)} %param.17), channel_id=1, source_target_pairs={{0,1},{1,0},{2,3},{3,2},{4,5},{5,4},{6,7},{7,6},{8,9},{9,8},{10,11... | collective-permute-start | bytes 12582920 | tf_op jit(solution)/shard_map/ppermute | solution.py:56
  36.1 12.3 %collective-permute-start.9 = (bf16[96,2176]{1,0:T(8,128)(2,1)}, bf16[96,2176]{1,0:T(8,128)(2,1)S(1)}, u32[]{:S(2)}, u32[]{:S(2)}) collective-permute-start(bf16[96,2176]{1,0:T(8,128)(2,1)} %get-tuple-element.67), channel_id=1, source_target_pairs={{0,2},{1,5},{2,0},{3,7},{4,6},{5,1},{6,4},{7,3},{8,10},{9,13},{10,... | collective-permute-start | bytes 1253384 | tf_op jit(solution)/shard_map/ppermute | solution.py:29
  36.6 11.7 %collective-permute-start.10 = (bf16[96,2176]{1,0:T(8,128)(2,1)S(1)}, bf16[96,2176]{1,0:T(8,128)(2,1)S(1)}, u32[]{:S(2)}, u32[]{:S(2)}) collective-permute-start(bf16[96,2176]{1,0:T(8,128)(2,1)S(1)} %get-tuple-element.68), channel_id=1, source_target_pairs={{0,4},{1,3},{2,6},{3,1},{4,0},{5,7},{6,2},{7,5},{8,12},{9,11},{10,... | collective-permute-start | bytes 1253384 | tf_op jit(solution)/shard_map/ppermute | solution.py:29
  37.2 10.5 %collective-permute-start.7 = (bf16[64,2176]{1,0:T(8,128)(2,1)S(1)}, bf16[64,2176]{1,0:T(8,128)(2,1)}, u32[]{:S(2)}, u32[]{:S(2)}) collective-permute-start(bf16[64,2176]{1,0:T(8,128)(2,1)S(1)} %collective-permute-done.2), channel_id=1, source_target_pairs={{8,0},{9,1},{10,2},{11,3},{12,4},{13,5},{14,6},{15,7},{16,24},{17,... | collective-permute-start | bytes 835592 | tf_op jit(solution)/shard_map/ppermute | solution.py:29
  38.4 9.2 %collective-permute-start.8 = (bf16[64,2176]{1,0:T(8,128)(2,1)S(1)}, bf16[64,2176]{1,0:T(8,128)(2,1)}, u32[]{:S(2)}, u32[]{:S(2)}) collective-permute-start(bf16[64,2176]{1,0:T(8,128)(2,1)S(1)} %collective-permute-done.3.refs_3_), channel_id=1, source_target_pairs={{8,16},{9,17},{10,18},{11,19},{12,20},{13,21},{14,22},{15,23},{16,... | collective-permute-start | bytes 835592 | tf_op jit(solution)/shard_map/ppermute | solution.py:29
  49.6 18.2 %collective-permute-start.12 = (bf16[160,2176]{1,0:T(8,128)(2,1)S(1)}, bf16[160,2176]{1,0:T(8,128)(2,1)S(1)}, u32[]{:S(2)}, u32[]{:S(2)}) collective-permute-start(bf16[160,2176]{1,0:T(8,128)(2,1)S(1)} %get-tuple-element.74), channel_id=1, source_target_pairs={{0,2},{1,5},{2,0},{3,7},{4,6},{5,1},{6,4},{7,3},{8,10},{9,13},{10,... | collective-permute-start | bytes 2088968 | tf_op jit(solution)/shard_map/ppermute | solution.py:29
  50.4 17.4 %collective-permute-start.13 = (bf16[160,2176]{1,0:T(8,128)(2,1)S(1)}, bf16[160,2176]{1,0:T(8,128)(2,1)S(1)}, u32[]{:S(2)}, u32[]{:S(2)}) collective-permute-start(bf16[160,2176]{1,0:T(8,128)(2,1)S(1)} %get-tuple-element.75), channel_id=1, source_target_pairs={{0,4},{1,3},{2,6},{3,1},{4,0},{5,7},{6,2},{7,5},{8,12},{9,11},{10,... | collective-permute-start | bytes 2088968 | tf_op jit(solution)/shard_map/ppermute | solution.py:29
  68.0 9.1 %collective-permute-start.14 = (bf16[64,2176]{1,0:T(8,128)(2,1)S(1)}, bf16[64,2176]{1,0:T(8,128)(2,1)S(1)}, u32[]{:S(2)}, u32[]{:S(2)}) collective-permute-start(bf16[64,2176]{1,0:T(8,128)(2,1)S(1)} %pad_maximum_fusion.9), channel_id=1, source_target_pairs={{0,2},{1,5},{2,0},{3,7},{4,6},{5,1},{6,4},{7,3},{8,10},{9,13},{10,... | collective-permute-start | bytes 835592 | tf_op jit(solution)/shard_map/ppermute | solution.py:29
  68.8 8.2 %collective-permute-start.15 = (bf16[64,2176]{1,0:T(8,128)(2,1)S(1)}, bf16[64,2176]{1,0:T(8,128)(2,1)S(1)}, u32[]{:S(2)}, u32[]{:S(2)}) collective-permute-start(bf16[64,2176]{1,0:T(8,128)(2,1)S(1)} %pad_maximum_fusion.10), channel_id=1, source_target_pairs={{0,4},{1,3},{2,6},{3,1},{4,0},{5,7},{6,2},{7,5},{8,12},{9,11},{10,... | collective-permute-start | bytes 835592 | tf_op jit(solution)/shard_map/ppermute | solution.py:29
  86.9 8.2 %collective-permute-start.16 = (bf16[64,2048]{1,0:T(8,128)(2,1)S(1)}, bf16[64,2048]{1,0:T(8,128)(2,1)S(1)}, u32[]{:S(2)}, u32[]{:S(2)}) collective-permute-start(bf16[64,2048]{1,0:T(8,128)(2,1)S(1)} %get-tuple-element.98), channel_id=1, source_target_pairs={{0,4},{1,3},{2,6},{3,1},{4,0},{5,7},{6,2},{7,5},{8,12},{9,11},{10,... | collective-permute-start | bytes 786440 | tf_op jit(solution)/shard_map/ppermute | solution.py:29
  88.1 8.3 %collective-permute-start.17 = (bf16[64,2048]{1,0:T(8,128)(2,1)S(1)}, bf16[64,2048]{1,0:T(8,128)(2,1)S(1)}, u32[]{:S(2)}, u32[]{:S(2)}) collective-permute-start(bf16[64,2048]{1,0:T(8,128)(2,1)S(1)} %get-tuple-element.100), channel_id=1, source_target_pairs={{0,2},{1,5},{2,0},{3,7},{4,6},{5,1},{6,4},{7,3},{8,10},{9,13},{10,... | collective-permute-start | bytes 786440 | tf_op jit(solution)/shard_map/ppermute | solution.py:29
  95.1 7.8 %collective-permute-start.18 = (bf16[64,2048]{1,0:T(8,128)(2,1)S(1)}, bf16[64,2048]{1,0:T(8,128)(2,1)S(1)}, u32[]{:S(2)}, u32[]{:S(2)}) collective-permute-start(bf16[64,2048]{1,0:T(8,128)(2,1)S(1)} %pad_maximum_fusion.11), channel_id=1, source_target_pairs={{0,2},{1,5},{2,0},{3,7},{4,6},{5,1},{6,4},{7,3},{8,10},{9,13},{10,... | collective-permute-start | bytes 786440 | tf_op jit(solution)/shard_map/ppermute | solution.py:29
  96.5 6.5 %collective-permute-start.19 = (bf16[64,2048]{1,0:T(8,128)(2,1)S(1)}, bf16[64,2048]{1,0:T(8,128)(2,1)S(1)}, u32[]{:S(2)}, u32[]{:S(2)}) collective-permute-start(bf16[64,2048]{1,0:T(8,128)(2,1)S(1)} %pad_maximum_fusion.12), channel_id=1, source_target_pairs={{0,4},{1,3},{2,6},{3,1},{4,0},{5,7},{6,2},{7,5},{8,12},{9,11},{10,... | collective-permute-start | bytes 786440 | tf_op jit(solution)/shard_map/ppermute | solution.py:29
  103.0 11.2 %collective-permute-start.20 = (bf16[96,2048]{1,0:T(8,128)(2,1)S(1)}, bf16[96,2048]{1,0:T(8,128)(2,1)S(1)}, u32[]{:S(2)}, u32[]{:S(2)}) collective-permute-start(bf16[96,2048]{1,0:T(8,128)(2,1)S(1)} %pad_maximum_fusion.5), channel_id=1, source_target_pairs={{0,2},{1,5},{2,0},{3,7},{4,6},{5,1},{6,4},{7,3},{8,10},{9,13},{10,... | collective-permute-start | bytes 1179656 | tf_op jit(solution)/shard_map/ppermute | solution.py:29
  104.8 25.4 %collective-permute-start.26 = (bf16[64,2048]{1,0:T(8,128)(2,1)S(1)}, bf16[64,2048]{1,0:T(8,128)(2,1)S(1)}, u32[]{:S(2)}, u32[]{:S(2)}) collective-permute-start(bf16[64,2048]{1,0:T(8,128)(2,1)S(1)} %add_convert_fusion.1), channel_id=1, source_target_pairs={{0,24},{1,25},{2,26},{3,27},{4,28},{5,29},{6,30},{7,31},{8,16},{9,... | collective-permute-start | bytes 786440 | tf_op jit(solution)/shard_map/ppermute | solution.py:29
  106.3 10.6 %collective-permute-start.23 = (bf16[96,2048]{1,0:T(8,128)(2,1)S(1)}, bf16[96,2048]{1,0:T(8,128)(2,1)S(1)}, u32[]{:S(2)}, u32[]{:S(2)}) collective-permute-start(bf16[96,2048]{1,0:T(8,128)(2,1)S(1)} %pad_maximum_fusion.6), channel_id=1, source_target_pairs={{0,4},{1,3},{2,6},{3,1},{4,0},{5,7},{6,2},{7,5},{8,12},{9,11},{10,... | collective-permute-start | bytes 1179656 | tf_op jit(solution)/shard_map/ppermute | solution.py:29
  114.2 24.1 %copy-start.1 = (bf16[128,1024]{1,0:T(8,128)(2,1)S(1)}, bf16[128,1024]{1,0:T(8,128)(2,1)}, u32[]{:S(2)}) copy-start(bf16[128,1024]{1,0:T(8,128)(2,1)} %param.9) | copy-start | bytes 786436
  114.3 12.4 %collective-permute-start.21 = (bf16[96,2048]{1,0:T(8,128)(2,1)S(1)}, bf16[96,2048]{1,0:T(8,128)(2,1)S(1)}, u32[]{:S(2)}, u32[]{:S(2)}) collective-permute-start(bf16[96,2048]{1,0:T(8,128)(2,1)S(1)} %pad_maximum_fusion.7), channel_id=1, source_target_pairs={{0,4},{1,3},{2,6},{3,1},{4,0},{5,7},{6,2},{7,5},{8,12},{9,11},{10,... | collective-permute-start | bytes 1179656 | tf_op jit(solution)/shard_map/ppermute | solution.py:29
  117.0 8.8 %collective-permute-start.27 = (bf16[64,2048]{1,0:T(8,128)(2,1)S(1)}, bf16[64,2048]{1,0:T(8,128)(2,1)S(1)}, u32[]{:S(2)}, u32[]{:S(2)}) collective-permute-start(bf16[64,2048]{1,0:T(8,128)(2,1)S(1)} %fusion.8), channel_id=1, source_target_pairs={{0,8},{1,9},{2,10},{3,11},{4,12},{5,13},{6,14},{7,15},{24,16},{25,... | collective-permute-start | bytes 786440 | tf_op jit(solution)/shard_map/ppermute | solution.py:29
  121.4 7.8 %collective-permute-start.24 = (bf16[96,2048]{1,0:T(8,128)(2,1)S(1)}, bf16[96,2048]{1,0:T(8,128)(2,1)S(1)}, u32[]{:S(2)}, u32[]{:S(2)}) collective-permute-start(bf16[96,2048]{1,0:T(8,128)(2,1)S(1)} %pad_maximum_fusion.8), channel_id=1, source_target_pairs={{0,2},{1,5},{2,0},{3,7},{4,6},{5,1},{6,4},{7,3},{8,10},{9,13},{10,... | collective-permute-start | bytes 1179656 | tf_op jit(solution)/shard_map/ppermute | solution.py:29
  126.0 6.2 %collective-permute-start.28 = (bf16[64,2048]{1,0:T(8,128)(2,1)S(1)}, bf16[64,2048]{1,0:T(8,128)(2,1)S(1)}, u32[]{:S(2)}, u32[]{:S(2)}) collective-permute-start(bf16[64,2048]{1,0:T(8,128)(2,1)S(1)} %add_convert_fusion), channel_id=1, source_target_pairs={{8,16},{9,17},{10,18},{11,19},{12,20},{13,21},{14,22},{15,23},{16,... | collective-permute-start | bytes 786440 | tf_op jit(solution)/shard_map/ppermute | solution.py:29
  126.7 8.6 %collective-permute-start.22 = (bf16[64,2048]{1,0:T(8,128)(2,1)S(1)}, bf16[64,2048]{1,0:T(8,128)(2,1)S(1)}, u32[]{:S(2)}, u32[]{:S(2)}) collective-permute-start(bf16[64,2048]{1,0:T(8,128)(2,1)S(1)} %pad_maximum_fusion.13), channel_id=1, source_target_pairs={{0,2},{1,5},{2,0},{3,7},{4,6},{5,1},{6,4},{7,3},{8,10},{9,13},{10,... | collective-permute-start | bytes 786440 | tf_op jit(solution)/shard_map/ppermute | solution.py:29
  129.3 6.4 %collective-permute-start.25 = (bf16[64,2048]{1,0:T(8,128)(2,1)S(1)}, bf16[64,2048]{1,0:T(8,128)(2,1)S(1)}, u32[]{:S(2)}, u32[]{:S(2)}) collective-permute-start(bf16[64,2048]{1,0:T(8,128)(2,1)S(1)} %pad_maximum_fusion.14), channel_id=1, source_target_pairs={{0,4},{1,3},{2,6},{3,1},{4,0},{5,7},{6,2},{7,5},{8,12},{9,11},{10,... | collective-permute-start | bytes 786440 | tf_op jit(solution)/shard_map/ppermute | solution.py:29
  130.3 7.0 %collective-permute-start.29 = (bf16[64,2048]{1,0:T(8,128)(2,1)S(1)}, bf16[64,2048]{1,0:T(8,128)(2,1)S(1)}, u32[]{:S(2)}, u32[]{:S(2)}) collective-permute-start(bf16[64,2048]{1,0:T(8,128)(2,1)S(1)} %fusion.7), channel_id=1, source_target_pairs={{0,8},{1,9},{2,10},{3,11},{4,12},{5,13},{6,14},{7,15},{8,0},{9,1},... | collective-permute-start | bytes 786440 | tf_op jit(solution)/shard_map/ppermute | solution.py:29
  (4 other events, 20.5 us)

commit v2 on v1

--- a/solution.py
+++ b/solution.py
@@ -92,10 +92,12 @@
 
 
 def collect(first, second):
-    own, x0, y0, pair, x1, y1 = first
-    far1, far2, x_far1, x_far2, y_far1, y_far2, x3, y3 = second
+    own, pair, far1, x1, x0, y1, y0, lo_x, lo_y = first
+    x_far1, x_far2, y_far1, y_far2, x3, y3, far2 = second
     rows = own.shape[0]
     half = rows // 2
+    z = lax.axis_index("req") // 4
+    middle = (z == 1) | (z == 2)
 
     def low(value, term):
         return joined(narrow(wide(value[:half]) + wide(term)), value[half:])
@@ -105,28 +107,32 @@
             value[:half], narrow(wide(value[half:rows]) + wide(term)), value[rows:]
         )
 
-    z = lax.axis_index("req") // 4
-    middle = (z == 1) | (z == 2)
     by_x = send(x3, ACROSS_X)
     by_y = send(y3, ACROSS_Y)
     x_sum = send(high(x_far2, by_y[half:]), ACROSS_X)
     y_sum = send(low(y_far2, by_x[half:]), ACROSS_Y)
     x_far1, y_far1 = high(x_far1, by_y[:half]), low(y_far1, by_x[:half])
     x_far1, y_far1, x_sum, y_sum = together(x_far1, y_far1, x_sum, y_sum)
-    next_ = send(narrow(wide(far2) + wide(x_sum) + wide(y_sum)), OPPOSITE_Z)
+    to_x = joined(wide(x1) + wide(y_sum[rows:]), wide(x0) + wide(lo_y[:half]))
+    to_y = joined(wide(y1) + wide(x_sum[rows:]), wide(y0) + wide(lo_x[:half]))
+    far2 = wide(far2) + wide(x_sum[:rows]) + wide(y_sum[:rows])
+    next_ = send(narrow(far2), OPPOSITE_Z)
     x_sum = send(x_far1, ACROSS_X)
     y_sum = send(y_far1, ACROSS_Y)
-    far1 = wide(far1) + wide(x_sum[:rows]) + wide(y_sum[:rows])
+    to_x, to_y, next_ = together(narrow(to_x), narrow(to_y), next_)
+    far1 = wide(far1) + wide(x_sum) + wide(y_sum)
     inward = send(narrow(far1), INWARD_Z)
     near = send(narrow(far1 + wide(inward)), MIDDLE_Z)
-    x_pair = send(high(x1, y_sum[rows:]), ACROSS_X)
-    y_pair = send(low(y1, x_sum[rows:]), ACROSS_Y)
-    pair = wide(pair) + wide(x_pair[:rows]) + wide(y_pair[:rows])
-    pair = narrow(pair + jnp.where(middle, wide(next_), 0.0))
-    by_pair = send(pair, PAIR_Z)
-    x_own = send(high(x0, y_pair[rows:]), ACROSS_X)
-    y_own = send(low(y0, x_pair[rows:]), ACROSS_Y)
-    total = wide(own) + wide(x_own) + wide(y_own) + jnp.where(middle, 0.0, wide(next_))
+    hi_x = send(to_x, ACROSS_X)
+    hi_y = send(to_y, ACROSS_Y)
+
+    def halves(i):
+        old, new = slice((i + 1) * half, (i + 2) * half), slice(i * half, (i + 1) * half)
+        return joined(wide(lo_x[old]) + wide(hi_y[new]), wide(hi_x[new]) + wide(lo_y[old]))
+
+    pair = wide(pair) + halves(0) + jnp.where(middle, wide(next_), 0.0)
+    by_pair = send(narrow(pair), PAIR_Z)
+    total = wide(own) + halves(1) + jnp.where(middle, 0.0, wide(next_))
     return total + wide(near) + wide(by_pair)
 
 
@@ -327,29 +333,36 @@
     far = tuple(w.reshape(-1, width) for w in far)
     run = functools.partial(run_experts, router=router_weight, local=local)
     takes = tuple((i, 0, rows) for i in range(7)) + ((4, rows, half), (5, rows, half))
-    gives = tuple(((i * rows, rows),) for i in range(4))
-    gives += (((4 * rows, rows), (7 * rows, half)),)
-    gives += (((5 * rows, rows), (7 * rows + half, half)),)
-    gives += (((6 * rows, rows),),)
+
+    def part(block, at):
+        return (block * rows + at, half)
+
+    gives = tuple(((i * rows, rows),) for i in (0, 3, 6))
+    gives += ((part(4, half),), (part(1, half),), (part(5, 0),), (part(2, 0),))
+    gives += ((part(7, 0), part(4, 0), part(1, 0)),)
+    gives += ((part(7, half), part(5, half), part(2, half)),)
     *done, ups, downs = run(first + [far1], takes, gives, weights=(*own, *far), loads=True)
     x2, y2, *done = lax.optimization_barrier((x2, y2, *done))
     x3, y3 = spread_last(x2, y2, rows)
-    first, (far1,) = done[:6], done[6:]
+    *first, lo_x, lo_y = done
+    lo_x = send(lo_x, ACROSS_X)
+    lo_y = send(lo_y, ACROSS_Y)
     takes = ((0, 0, 2 * rows), (1, 0, 2 * rows), (0, 2 * rows, half), (1, 2 * rows, half))
     takes += ((2, 0, half), (3, 0, half), (2, half, half), (3, half, half), (4, 0, rows))
     gives = (
-        ((0, rows), (4 * rows, half)),
-        ((rows, rows),),
-        ((2 * rows, rows), (4 * rows + half, half)),
-        ((3 * rows, rows),),
-        ((5 * rows, half), (6 * rows, half)),
-        ((5 * rows + half, half), (6 * rows + half, half)),
+        ((0, rows),),
+        ((rows, rows), part(4, 0)),
+        ((2 * rows, rows),),
+        ((3 * rows, rows), part(4, half)),
+        (part(5, 0), part(6, 0)),
+        (part(5, half), part(6, half)),
         ((7 * rows, rows),),
     )
-    *second, far2 = run(
+    second = run(
         [x2, y2, x3, y3, far2], takes, gives, weights=(ups, downs), loads=False
     )
-    second = [far1, far2, *second]
+    lo_x, lo_y, *second = lax.optimization_barrier((lo_x, lo_y, *second))
+    first = [*first, lo_x, lo_y]
     mix = collect(first, second)
     return (hidden_state.astype(jnp.bfloat16), mix.astype(jnp.bfloat16))
 

time: 139 us -> 135 us (0.971)
  waiting for transfers between devices: 62.4 us -> 57.8 us
    ppermute x26, waiting for transfers between devices: 58.2 us -> 53.6 us  [send(): return lax.ppermute(value, ('req', 'tp'), pairs)]
  transfers between devices with their start and end apart: 30 -> 30, of which waited for: 18 -> 17; matrix products, arithmetic and copies ran while one was open for 5% -> 5% of each run, Pallas kernels for 10% -> 17%
where the time goes in v2:
time: 135 us
  waiting for transfers between devices  57.8 us (43%)
  starting transfers between devices  39.2 us (29%)
  Pallas kernels  23 us (17%)
  matrix products  6.38 us (5%)
  other arithmetic  4.93 us (4%)
  local copies, waits for them, and re-layouts  2.37 us (2%)
    ppermute x26, waiting for transfers between devices, send(): return lax.ppermute(value, ('req', 'tp'), pairs)  53.6 us
    ppermute x26, starting transfers between devices, send(): return lax.ppermute(value, ('req', 'tp'), pairs)  37.9 us
    pallas_call x2, Pallas kernels, run_experts(): pl.pallas_call(functools.partial(expert_body, takes, gives, tile, group,...  23 us
    dot_general x1, matrix products, project(): kept = jnp.dot(ours, out_weight, preferred_element_type=jnp.float32)  3.18 us
    dot_general x1, matrix products, project(): sent = jnp.dot(theirs, out_weight, preferred_element_type=jnp.float32)  3.07 us
  transfers between devices with their start and end apart: 30, of which 17 were waited for; matrix products, arithmetic and copies ran while one was open for 5% of the time, Pallas kernels for 17%

profile of v2, /device:TPU:0, one launch (start us, length us, event | category | flops | bytes accessed | tf_op | source)
XLA Modules:
  0.0 134.6 jit_solution(2364046155765990913)
XLA Ops:
  1.6 3.1 %fusion.10 = f32[64,2048]{1,0:T(8,128)S(1)} fusion(bf16[1024,2048]{1,0:T(8,128)(2,1)} %param.10, bf16[128,1024]{1,0:T(8,128)(2,1)S(1)} %copy-done, s32[]{:T(128)S(6)} %select_n.39), kind=kOutput, calls=%fused_computation.50 | convolution fusion | flops 268435456 | bytes 4849668 | tf_op jit(solution)/shard_map/dot_general | solution.py:302
  5.2 1.5 %collective-permute-done = f32[64,2048]{1,0:T(8,128)S(1)} collective-permute-done((f32[64,2048]{1,0:T(8,128)S(1)}, f32[64,2048]{1,0:T(8,128)S(1)}, u32[]{:S(2)}, u32[]{:S(2)}) %collective-permute-start) | collective-permute-done | bytes 524320 | tf_op jit(solution)/shard_map/ppermute | solution.py:303
  7.4 3.2 %fusion.12 = f32[64,2048]{1,0:T(8,128)S(1)} fusion(bf16[1024,2048]{1,0:T(8,128)(2,1)} %param.10, bf16[128,1024]{1,0:T(8,128)(2,1)S(1)} %copy-done, s32[]{:T(128)S(6)} %select_n.38), kind=kOutput, calls=%fused_computation.52 | convolution fusion | flops 268435456 | bytes 4849668 | tf_op jit(solution)/shard_map/dot_general | solution.py:304
  11.6 2.7 %collective-permute-done.1 = bf16[2,512,2048]{2,1,0:T(8,128)(2,1)} collective-permute-done((bf16[2,512,2048]{2,1,0:T(8,128)(2,1)}, bf16[2,512,2048]{2,1,0:T(8,128)(2,1)}, u32[]{:S(2)}, u32[]{:S(2)}) %collective-permute-start.1) | collective-permute-done | bytes 4194336 | tf_op jit(solution)/shard_map/ppermute | solution.py:56
  14.6 2.7 %collective-permute-start.5 = (bf16[64,2176]{1,0:T(8,128)(2,1)S(1)}, bf16[64,2176]{1,0:T(8,128)(2,1)S(1)}, u32[]{:S(2)}, u32[]{:S(2)}) collective-permute-start(bf16[64,2176]{1,0:T(8,128)(2,1)S(1)} %fusion.9.refs_0_), channel_id=1, source_target_pairs={{0,4},{1,3},{2,6},{3,1},{4,0},{5,7},{6,2},{7,5},{8,12},{9,11},{10,... | collective-permute-start | bytes 835592 | tf_op jit(solution)/shard_map/ppermute | solution.py:29
  17.3 1.5 %collective-permute-start.4 = (bf16[64,2176]{1,0:T(8,128)(2,1)S(1)}, bf16[64,2176]{1,0:T(8,128)(2,1)S(1)}, u32[]{:S(2)}, u32[]{:S(2)}) collective-permute-start(bf16[64,2176]{1,0:T(8,128)(2,1)S(1)} %fusion.9.refs_0_), channel_id=1, source_target_pairs={{0,2},{1,5},{2,0},{3,7},{4,6},{5,1},{6,4},{7,3},{8,10},{9,13},{10,... | collective-permute-start | bytes 835592 | tf_op jit(solution)/shard_map/ppermute | solution.py:29
  18.8 1.6 %collective-permute-start.3 = (bf16[64,2176]{1,0:T(8,128)(2,1)S(1)}, bf16[64,2176]{1,0:T(8,128)(2,1)S(1)}, u32[]{:S(2)}, u32[]{:S(2)}) collective-permute-start(bf16[64,2176]{1,0:T(8,128)(2,1)S(1)} %fusion.9.refs_0_), channel_id=1, source_target_pairs={{0,8},{1,9},{2,10},{3,11},{4,12},{5,13},{6,14},{7,15},{8,0},{9,1},... | collective-permute-start | bytes 835592 | tf_op jit(solution)/shard_map/ppermute | solution.py:29
  20.3 2.5 %collective-permute-start.2 = (bf16[64,2176]{1,0:T(8,128)(2,1)S(1)}, bf16[64,2176]{1,0:T(8,128)(2,1)S(1)}, u32[]{:S(2)}, u32[]{:S(2)}) collective-permute-start(bf16[64,2176]{1,0:T(8,128)(2,1)S(1)} %fusion.9.refs_0_), channel_id=1, source_target_pairs={{0,24},{1,25},{2,26},{3,27},{4,28},{5,29},{6,30},{7,31},{8,16},{9,... | collective-permute-start | bytes 835592 | tf_op jit(solution)/shard_map/ppermute | solution.py:29
  24.4 3.0 %collective-permute-done.3.refs_3_ = bf16[64,2176]{1,0:T(8,128)(2,1)S(1)} collective-permute-done((bf16[64,2176]{1,0:T(8,128)(2,1)S(1)}, bf16[64,2176]{1,0:T(8,128)(2,1)S(1)}, u32[]{:S(2)}, u32[]{:S(2)}) %collective-permute-start.3) | collective-permute-done | bytes 278560 | tf_op jit(solution)/shard_map/ppermute | solution.py:29
  27.4 7.8 %collective-permute-done.2 = bf16[64,2176]{1,0:T(8,128)(2,1)S(1)} collective-permute-done((bf16[64,2176]{1,0:T(8,128)(2,1)S(1)}, bf16[64,2176]{1,0:T(8,128)(2,1)S(1)}, u32[]{:S(2)}, u32[]{:S(2)}) %collective-permute-start.2) | collective-permute-done | bytes 278560 | tf_op jit(solution)/shard_map/ppermute | solution.py:29
  37.2 1.3 collective-permute-start.7
  38.4 1.4 %collective-permute-start.8 = (bf16[64,2176]{1,0:T(8,128)(2,1)S(1)}, bf16[64,2176]{1,0:T(8,128)(2,1)}, u32[]{:S(2)}, u32[]{:S(2)}) collective-permute-start(bf16[64,2176]{1,0:T(8,128)(2,1)S(1)} %collective-permute-done.3.refs_3_), channel_id=1, source_target_pairs={{8,16},{9,17},{10,18},{11,19},{12,20},{13,21},{14,22},{15,23},{16,... | collective-permute-start | bytes 835592 | tf_op jit(solution)/shard_map/ppermute | solution.py:29
  41.1 6.6 %collective-permute-done.7 = bf16[64,2176]{1,0:T(8,128)(2,1)} collective-permute-done((bf16[64,2176]{1,0:T(8,128)(2,1)S(1)}, bf16[64,2176]{1,0:T(8,128)(2,1)}, u32[]{:S(2)}, u32[]{:S(2)}) %collective-permute-start.7) | collective-permute-done | bytes 278560 | tf_op jit(solution)/shard_map/ppermute | solution.py:29
  50.4 1.5 %collective-permute-start.13 = (bf16[160,2176]{1,0:T(8,128)(2,1)S(1)}, bf16[160,2176]{1,0:T(8,128)(2,1)S(1)}, u32[]{:S(2)}, u32[]{:S(2)}) collective-permute-start(bf16[160,2176]{1,0:T(8,128)(2,1)S(1)} %get-tuple-element.91), channel_id=1, source_target_pairs={{0,4},{1,3},{2,6},{3,1},{4,0},{5,7},{6,2},{7,5},{8,12},{9,11},{10,... | collective-permute-start | bytes 2088968 | tf_op jit(solution)/shard_map/ppermute | solution.py:29
  51.9 13.2 %shard_map.104 = (bf16[64,2048]{1,0:T(8,128)(2,1)S(1)}, bf16[64,2048]{1,0:T(8,128)(2,1)S(1)}, bf16[64,2048]{1,0:T(8,128)(2,1)S(1)}, bf16[32,2048]{1,0:T(8,128)(2...) custom-call(bf16[64,2176]{1,0:T(8,128)(2,1)S(1)} %fusion.9.refs_0_, ...), custom_call_target="tpu_custom_call" | custom-call | flops 8589934592 | bytes 29360128 | tf_op jit(solution)/shard_map/pallas_call | solution.py:274
  65.1 2.7 %collective-permute-done.12.refs_0_ = bf16[160,2176]{1,0:T(8,128)(2,1)S(1)} collective-permute-done((bf16[160,2176]{1,0:T(8,128)(2,1)S(1)}, bf16[160,2176]{1,0:T(8,128)(2,1)S(1)}, u32[]{:S(2)}, u32[]{:S(2)}) %collective-permute-start.12) | collective-permute-done | bytes 696352 | tf_op jit(solution)/shard_map/ppermute | solution.py:29
  69.5 1.4 %collective-permute-start.14 = (bf16[96,2048]{1,0:T(8,128)(2,1)S(1)}, bf16[96,2048]{1,0:T(8,128)(2,1)S(1)}, u32[]{:S(2)}, u32[]{:S(2)}) collective-permute-start(bf16[96,2048]{1,0:T(8,128)(2,1)S(1)} %get-tuple-element.106), channel_id=1, source_target_pairs={{0,2},{1,5},{2,0},{3,7},{4,6},{5,1},{6,4},{7,3},{8,10},{9,13},{10,... | collective-permute-start | bytes 1179656 | tf_op jit(solution)/shard_map/ppermute | solution.py:29
  72.0 5.4 %collective-permute-done.16.refs_2_ = bf16[64,2176]{1,0:T(8,128)(2,1)S(1)} collective-permute-done((bf16[64,2176]{1,0:T(8,128)(2,1)S(1)}, bf16[64,2176]{1,0:T(8,128)(2,1)S(1)}, u32[]{:S(2)}, u32[]{:S(2)}) %collective-permute-start.16) | collective-permute-done | bytes 278560 | tf_op jit(solution)/shard_map/ppermute | solution.py:29
  78.4 9.8 %shard_map.105 = (bf16[64,2048]{1,0:T(8,128)(2,1)S(1)}, bf16[96,2048]{1,0:T(8,128)(2,1)S(1)}, bf16[64,2048]{1,0:T(8,128)(2,1)S(1)}, bf16[96,2048]{1,0:T(8,128)(2...) custom-call(bf16[160,2176]{1,0:T(8,128)(2,1)S(1)} %collective-permute-done.12.refs, ...), custom_call_target="tpu_custom_call" | custom-call | flops 8589934592 | bytes 29360128 | tf_op jit(solution)/shard_map/pallas_call | solution.py:274
  89.0 1.4 %collective-permute-start.19 = (bf16[64,2048]{1,0:T(8,128)(2,1)S(1)}, bf16[64,2048]{1,0:T(8,128)(2,1)S(1)}, u32[]{:S(2)}, u32[]{:S(2)}) collective-permute-start(bf16[64,2048]{1,0:T(8,128)(2,1)S(1)} %get-tuple-element.127), channel_id=1, source_target_pairs={{0,2},{1,5},{2,0},{3,7},{4,6},{5,1},{6,4},{7,3},{8,10},{9,13},{10,... | collective-permute-start | bytes 786440 | tf_op jit(solution)/shard_map/ppermute | solution.py:29
  90.5 4.9 %collective-permute-done.19 = bf16[64,2048]{1,0:T(8,128)(2,1)S(1)} collective-permute-done((bf16[64,2048]{1,0:T(8,128)(2,1)S(1)}, bf16[64,2048]{1,0:T(8,128)(2,1)S(1)}, u32[]{:S(2)}, u32[]{:S(2)}) %collective-permute-start.19) | collective-permute-done | bytes 262176 | tf_op jit(solution)/shard_map/ppermute | solution.py:29
  95.5 1.4 %collective-permute-start.21 = (bf16[96,2048]{1,0:T(8,128)(2,1)S(1)}, bf16[96,2048]{1,0:T(8,128)(2,1)S(1)}, u32[]{:S(2)}, u32[]{:S(2)}) collective-permute-start(bf16[96,2048]{1,0:T(8,128)(2,1)S(1)} %pad_maximum_fusion.6), channel_id=1, source_target_pairs={{0,4},{1,3},{2,6},{3,1},{4,0},{5,7},{6,2},{7,5},{8,12},{9,11},{10,... | collective-permute-start | bytes 1179656 | tf_op jit(solution)/shard_map/ppermute | solution.py:29
  98.3 7.2 %collective-permute-done.21 = bf16[96,2048]{1,0:T(8,128)(2,1)S(1)} collective-permute-done((bf16[96,2048]{1,0:T(8,128)(2,1)S(1)}, bf16[96,2048]{1,0:T(8,128)(2,1)S(1)}, u32[]{:S(2)}, u32[]{:S(2)}) %collective-permute-start.21) | collective-permute-done | bytes 393248 | tf_op jit(solution)/shard_map/ppermute | solution.py:29
  106.7 1.7 %collective-permute-start.26 = (bf16[64,2048]{1,0:T(8,128)(2,1)S(1)}, bf16[64,2048]{1,0:T(8,128)(2,1)S(1)}, u32[]{:S(2)}, u32[]{:S(2)}) collective-permute-start(bf16[64,2048]{1,0:T(8,128)(2,1)S(1)} %pad_maximum_fusion.10), channel_id=1, source_target_pairs={{0,4},{1,3},{2,6},{3,1},{4,0},{5,7},{6,2},{7,5},{8,12},{9,11},{10,... | collective-permute-start | bytes 786440 | tf_op jit(solution)/shard_map/ppermute | solution.py:29
  108.5 1.5 %collective-permute-start.22 = (bf16[64,2048]{1,0:T(8,128)(2,1)S(1)}, bf16[64,2048]{1,0:T(8,128)(2,1)S(1)}, u32[]{:S(2)}, u32[]{:S(2)}) collective-permute-start(bf16[64,2048]{1,0:T(8,128)(2,1)S(1)} %add_convert_fusion.1), channel_id=1, source_target_pairs={{0,24},{1,25},{2,26},{3,27},{4,28},{5,29},{6,30},{7,31},{8,16},{9,... | collective-permute-start | bytes 786440 | tf_op jit(solution)/shard_map/ppermute | solution.py:29
  110.2 3.4 %collective-permute-done.25 = bf16[64,2048]{1,0:T(8,128)(2,1)S(1)} collective-permute-done((bf16[64,2048]{1,0:T(8,128)(2,1)S(1)}, bf16[64,2048]{1,0:T(8,128)(2,1)S(1)}, u32[]{:S(2)}, u32[]{:S(2)}) %collective-permute-start.25) | collective-permute-done | bytes 262176 | tf_op jit(solution)/shard_map/ppermute | solution.py:29
  113.7 4.9 %collective-permute-start.27 = (bf16[64,2048]{1,0:T(8,128)(2,1)S(1)}, bf16[64,2048]{1,0:T(8,128)(2,1)S(1)}, u32[]{:S(2)}, u32[]{:S(2)}) collective-permute-start(bf16[64,2048]{1,0:T(8,128)(2,1)S(1)} %fusion.8), channel_id=1, source_target_pairs={{0,8},{1,9},{2,10},{3,11},{4,12},{5,13},{6,14},{7,15},{24,16},{25,... | collective-permute-start | bytes 786440 | tf_op jit(solution)/shard_map/ppermute | solution.py:29
  118.7 2.1 %collective-permute-start.23 = (bf16[64,2048]{1,0:T(8,128)(2,1)S(1)}, bf16[64,2048]{1,0:T(8,128)(2,1)S(1)}, u32[]{:S(2)}, u32[]{:S(2)}) collective-permute-start(bf16[64,2048]{1,0:T(8,128)(2,1)S(1)} %pad_maximum_fusion.12), channel_id=1, source_target_pairs={{0,4},{1,3},{2,6},{3,1},{4,0},{5,7},{6,2},{7,5},{8,12},{9,11},{10,... | collective-permute-start | bytes 786440 | tf_op jit(solution)/shard_map/ppermute | solution.py:29
  120.8 2.0 %collective-permute-start.24 = (bf16[64,2048]{1,0:T(8,128)(2,1)S(1)}, bf16[64,2048]{1,0:T(8,128)(2,1)S(1)}, u32[]{:S(2)}, u32[]{:S(2)}) collective-permute-start(bf16[64,2048]{1,0:T(8,128)(2,1)S(1)} %pad_maximum_fusion.11), channel_id=1, source_target_pairs={{0,2},{1,5},{2,0},{3,7},{4,6},{5,1},{6,4},{7,3},{8,10},{9,13},{10,... | collective-permute-start | bytes 786440 | tf_op jit(solution)/shard_map/ppermute | solution.py:29
  123.6 1.5 %collective-permute-done.23 = bf16[64,2048]{1,0:T(8,128)(2,1)S(1)} collective-permute-done((bf16[64,2048]{1,0:T(8,128)(2,1)S(1)}, bf16[64,2048]{1,0:T(8,128)(2,1)S(1)}, u32[]{:S(2)}, u32[]{:S(2)}) %collective-permute-start.23) | collective-permute-done | bytes 262176 | tf_op jit(solution)/shard_map/ppermute | solution.py:29
  125.2 1.9 %collective-permute-done.24 = bf16[64,2048]{1,0:T(8,128)(2,1)S(1)} collective-permute-done((bf16[64,2048]{1,0:T(8,128)(2,1)S(1)}, bf16[64,2048]{1,0:T(8,128)(2,1)S(1)}, u32[]{:S(2)}, u32[]{:S(2)}) %collective-permute-start.24) | collective-permute-done | bytes 262176 | tf_op jit(solution)/shard_map/ppermute | solution.py:29
  127.9 5.9 %collective-permute-done.29 = bf16[64,2048]{1,0:T(8,128)(2,1)S(1)} collective-permute-done((bf16[64,2048]{1,0:T(8,128)(2,1)S(1)}, bf16[64,2048]{1,0:T(8,128)(2,1)S(1)}, u32[]{:S(2)}, u32[]{:S(2)}) %collective-permute-start.29) | collective-permute-done | bytes 262176 | tf_op jit(solution)/shard_map/ppermute | solution.py:29
  (87 shorter events, 21.1 us)
Async XLA Ops:
  1.6 9.0 %copy-start.2 = (bf16[64,2048]{1,0:T(8,128)(2,1)S(1)}, bf16[64,2048]{1,0:T(8,128)(2,1)}, u32[]{:S(2)}) copy-start(bf16[64,2048]{1,0:T(8,128)(2,1)} %param.11) | copy-start | bytes 786436
  4.7 2.1 %collective-permute-start = (f32[64,2048]{1,0:T(8,128)S(1)}, f32[64,2048]{1,0:T(8,128)S(1)}, u32[]{:S(2)}, u32[]{:S(2)}) collective-permute-start(f32[64,2048]{1,0:T(8,128)S(1)} %fusion.10), channel_id=1, source_target_pairs={{0,1},{1,0},{2,3},{3,2},{4,5},{5,4},{6,7},{7,6},{8,9},{9,8},{10,11... | collective-permute-start | bytes 1572872 | tf_op jit(solution)/shard_map/ppermute | solution.py:303
  6.7 7.5 %collective-permute-start.1 = (bf16[2,512,2048]{2,1,0:T(8,128)(2,1)}, bf16[2,512,2048]{2,1,0:T(8,128)(2,1)}, u32[]{:S(2)}, u32[]{:S(2)}) collective-permute-start(bf16[2,512,2048]{2,1,0:T(8,128)(2,1)} %param.15), channel_id=1, source_target_pairs={{0,1},{1,0},{2,3},{3,2},{4,5},{5,4},{6,7},{7,6},{8,9},{9,8},{10,11... | collective-permute-start | bytes 12582920 | tf_op jit(solution)/shard_map/ppermute | solution.py:56
  14.2 21.0 %collective-permute-start.6 = (bf16[2,512,2048]{2,1,0:T(8,128)(2,1)S(1)}, bf16[2,512,2048]{2,1,0:T(8,128)(2,1)}, u32[]{:S(2)}, u32[]{:S(2)}) collective-permute-start(bf16[2,512,2048]{2,1,0:T(8,128)(2,1)S(1)} %copy-done.5), channel_id=1, source_target_pairs={{0,1},{1,0},{2,3},{3,2},{4,5},{5,4},{6,7},{7,6},{8,9},{9,8},{10,11... | collective-permute-start | bytes 12582920 | tf_op jit(solution)/shard_map/ppermute | solution.py:56
  14.6 9.1 %collective-permute-start.5 = (bf16[64,2176]{1,0:T(8,128)(2,1)S(1)}, bf16[64,2176]{1,0:T(8,128)(2,1)S(1)}, u32[]{:S(2)}, u32[]{:S(2)}) collective-permute-start(bf16[64,2176]{1,0:T(8,128)(2,1)S(1)} %fusion.9.refs_0_), channel_id=1, source_target_pairs={{0,4},{1,3},{2,6},{3,1},{4,0},{5,7},{6,2},{7,5},{8,12},{9,11},{10,... | collective-permute-start | bytes 835592 | tf_op jit(solution)/shard_map/ppermute | solution.py:29
  17.3 7.2 %collective-permute-start.4 = (bf16[64,2176]{1,0:T(8,128)(2,1)S(1)}, bf16[64,2176]{1,0:T(8,128)(2,1)S(1)}, u32[]{:S(2)}, u32[]{:S(2)}) collective-permute-start(bf16[64,2176]{1,0:T(8,128)(2,1)S(1)} %fusion.9.refs_0_), channel_id=1, source_target_pairs={{0,2},{1,5},{2,0},{3,7},{4,6},{5,1},{6,4},{7,3},{8,10},{9,13},{10,... | collective-permute-start | bytes 835592 | tf_op jit(solution)/shard_map/ppermute | solution.py:29
  18.8 8.6 %collective-permute-start.3 = (bf16[64,2176]{1,0:T(8,128)(2,1)S(1)}, bf16[64,2176]{1,0:T(8,128)(2,1)S(1)}, u32[]{:S(2)}, u32[]{:S(2)}) collective-permute-start(bf16[64,2176]{1,0:T(8,128)(2,1)S(1)} %fusion.9.refs_0_), channel_id=1, source_target_pairs={{0,8},{1,9},{2,10},{3,11},{4,12},{5,13},{6,14},{7,15},{8,0},{9,1},... | collective-permute-start | bytes 835592 | tf_op jit(solution)/shard_map/ppermute | solution.py:29
  20.3 14.9 %collective-permute-start.2 = (bf16[64,2176]{1,0:T(8,128)(2,1)S(1)}, bf16[64,2176]{1,0:T(8,128)(2,1)S(1)}, u32[]{:S(2)}, u32[]{:S(2)}) collective-permute-start(bf16[64,2176]{1,0:T(8,128)(2,1)S(1)} %fusion.9.refs_0_), channel_id=1, source_target_pairs={{0,24},{1,25},{2,26},{3,27},{4,28},{5,29},{6,30},{7,31},{8,16},{9,... | collective-permute-start | bytes 835592 | tf_op jit(solution)/shard_map/ppermute | solution.py:29
  36.1 12.3 %collective-permute-start.11 = (bf16[2,512,2048]{2,1,0:T(8,128)(2,1)}, bf16[2,512,2048]{2,1,0:T(8,128)(2,1)}, u32[]{:S(2)}, u32[]{:S(2)}) collective-permute-start(bf16[2,512,2048]{2,1,0:T(8,128)(2,1)} %param.17), channel_id=1, source_target_pairs={{0,1},{1,0},{2,3},{3,2},{4,5},{5,4},{6,7},{7,6},{8,9},{9,8},{10,11... | collective-permute-start | bytes 12582920 | tf_op jit(solution)/shard_map/ppermute | solution.py:56
  36.1 12.3 %collective-permute-start.9 = (bf16[96,2176]{1,0:T(8,128)(2,1)}, bf16[96,2176]{1,0:T(8,128)(2,1)S(1)}, u32[]{:S(2)}, u32[]{:S(2)}) collective-permute-start(bf16[96,2176]{1,0:T(8,128)(2,1)} %get-tuple-element.83), channel_id=1, source_target_pairs={{0,2},{1,5},{2,0},{3,7},{4,6},{5,1},{6,4},{7,3},{8,10},{9,13},{10,... | collective-permute-start | bytes 1253384 | tf_op jit(solution)/shard_map/ppermute | solution.py:29
  36.6 11.7 %collective-permute-start.10 = (bf16[96,2176]{1,0:T(8,128)(2,1)S(1)}, bf16[96,2176]{1,0:T(8,128)(2,1)S(1)}, u32[]{:S(2)}, u32[]{:S(2)}) collective-permute-start(bf16[96,2176]{1,0:T(8,128)(2,1)S(1)} %get-tuple-element.84), channel_id=1, source_target_pairs={{0,4},{1,3},{2,6},{3,1},{4,0},{5,7},{6,2},{7,5},{8,12},{9,11},{10,... | collective-permute-start | bytes 1253384 | tf_op jit(solution)/shard_map/ppermute | solution.py:29
  37.2 10.5 %collective-permute-start.7 = (bf16[64,2176]{1,0:T(8,128)(2,1)S(1)}, bf16[64,2176]{1,0:T(8,128)(2,1)}, u32[]{:S(2)}, u32[]{:S(2)}) collective-permute-start(bf16[64,2176]{1,0:T(8,128)(2,1)S(1)} %collective-permute-done.2), channel_id=1, source_target_pairs={{8,0},{9,1},{10,2},{11,3},{12,4},{13,5},{14,6},{15,7},{16,24},{17,... | collective-permute-start | bytes 835592 | tf_op jit(solution)/shard_map/ppermute | solution.py:29
  38.4 9.2 %collective-permute-start.8 = (bf16[64,2176]{1,0:T(8,128)(2,1)S(1)}, bf16[64,2176]{1,0:T(8,128)(2,1)}, u32[]{:S(2)}, u32[]{:S(2)}) collective-permute-start(bf16[64,2176]{1,0:T(8,128)(2,1)S(1)} %collective-permute-done.3.refs_3_), channel_id=1, source_target_pairs={{8,16},{9,17},{10,18},{11,19},{12,20},{13,21},{14,22},{15,23},{16,... | collective-permute-start | bytes 835592 | tf_op jit(solution)/shard_map/ppermute | solution.py:29
  49.6 18.2 %collective-permute-start.12 = (bf16[160,2176]{1,0:T(8,128)(2,1)S(1)}, bf16[160,2176]{1,0:T(8,128)(2,1)S(1)}, u32[]{:S(2)}, u32[]{:S(2)}) collective-permute-start(bf16[160,2176]{1,0:T(8,128)(2,1)S(1)} %get-tuple-element.90), channel_id=1, source_target_pairs={{0,2},{1,5},{2,0},{3,7},{4,6},{5,1},{6,4},{7,3},{8,10},{9,13},{10,... | collective-permute-start | bytes 2088968 | tf_op jit(solution)/shard_map/ppermute | solution.py:29
  50.4 17.4 %collective-permute-start.13 = (bf16[160,2176]{1,0:T(8,128)(2,1)S(1)}, bf16[160,2176]{1,0:T(8,128)(2,1)S(1)}, u32[]{:S(2)}, u32[]{:S(2)}) collective-permute-start(bf16[160,2176]{1,0:T(8,128)(2,1)S(1)} %get-tuple-element.91), channel_id=1, source_target_pairs={{0,4},{1,3},{2,6},{3,1},{4,0},{5,7},{6,2},{7,5},{8,12},{9,11},{10,... | collective-permute-start | bytes 2088968 | tf_op jit(solution)/shard_map/ppermute | solution.py:29
  67.9 9.5 %collective-permute-start.16 = (bf16[64,2176]{1,0:T(8,128)(2,1)S(1)}, bf16[64,2176]{1,0:T(8,128)(2,1)S(1)}, u32[]{:S(2)}, u32[]{:S(2)}) collective-permute-start(bf16[64,2176]{1,0:T(8,128)(2,1)S(1)} %pad_maximum_fusion.7), channel_id=1, source_target_pairs={{0,2},{1,5},{2,0},{3,7},{4,6},{5,1},{6,4},{7,3},{8,10},{9,13},{10,... | collective-permute-start | bytes 835592 | tf_op jit(solution)/shard_map/ppermute | solution.py:29
  68.8 9.6 %collective-permute-start.17 = (bf16[64,2176]{1,0:T(8,128)(2,1)S(1)}, bf16[64,2176]{1,0:T(8,128)(2,1)S(1)}, u32[]{:S(2)}, u32[]{:S(2)}) collective-permute-start(bf16[64,2176]{1,0:T(8,128)(2,1)S(1)} %pad_maximum_fusion.8), channel_id=1, source_target_pairs={{0,4},{1,3},{2,6},{3,1},{4,0},{5,7},{6,2},{7,5},{8,12},{9,11},{10,... | collective-permute-start | bytes 835592 | tf_op jit(solution)/shard_map/ppermute | solution.py:29
  69.5 18.7 %collective-permute-start.14 = (bf16[96,2048]{1,0:T(8,128)(2,1)S(1)}, bf16[96,2048]{1,0:T(8,128)(2,1)S(1)}, u32[]{:S(2)}, u32[]{:S(2)}) collective-permute-start(bf16[96,2048]{1,0:T(8,128)(2,1)S(1)} %get-tuple-element.106), channel_id=1, source_target_pairs={{0,2},{1,5},{2,0},{3,7},{4,6},{5,1},{6,4},{7,3},{8,10},{9,13},{10,... | collective-permute-start | bytes 1179656 | tf_op jit(solution)/shard_map/ppermute | solution.py:29
  70.9 17.3 %collective-permute-start.15 = (bf16[96,2048]{1,0:T(8,128)(2,1)S(1)}, bf16[96,2048]{1,0:T(8,128)(2,1)S(1)}, u32[]{:S(2)}, u32[]{:S(2)}) collective-permute-start(bf16[96,2048]{1,0:T(8,128)(2,1)S(1)} %get-tuple-element.107), channel_id=1, source_target_pairs={{0,4},{1,3},{2,6},{3,1},{4,0},{5,7},{6,2},{7,5},{8,12},{9,11},{10,... | collective-permute-start | bytes 1179656 | tf_op jit(solution)/shard_map/ppermute | solution.py:29
  88.3 8.6 %collective-permute-start.18 = (bf16[64,2048]{1,0:T(8,128)(2,1)S(1)}, bf16[64,2048]{1,0:T(8,128)(2,1)S(1)}, u32[]{:S(2)}, u32[]{:S(2)}) collective-permute-start(bf16[64,2048]{1,0:T(8,128)(2,1)S(1)} %get-tuple-element.125), channel_id=1, source_target_pairs={{0,4},{1,3},{2,6},{3,1},{4,0},{5,7},{6,2},{7,5},{8,12},{9,11},{10,... | collective-permute-start | bytes 786440 | tf_op jit(solution)/shard_map/ppermute | solution.py:29
  89.0 6.4 %collective-permute-start.19 = (bf16[64,2048]{1,0:T(8,128)(2,1)S(1)}, bf16[64,2048]{1,0:T(8,128)(2,1)S(1)}, u32[]{:S(2)}, u32[]{:S(2)}) collective-permute-start(bf16[64,2048]{1,0:T(8,128)(2,1)S(1)} %get-tuple-element.127), channel_id=1, source_target_pairs={{0,2},{1,5},{2,0},{3,7},{4,6},{5,1},{6,4},{7,3},{8,10},{9,13},{10,... | collective-permute-start | bytes 786440 | tf_op jit(solution)/shard_map/ppermute | solution.py:29
  95.5 10.0 %collective-permute-start.21 = (bf16[96,2048]{1,0:T(8,128)(2,1)S(1)}, bf16[96,2048]{1,0:T(8,128)(2,1)S(1)}, u32[]{:S(2)}, u32[]{:S(2)}) collective-permute-start(bf16[96,2048]{1,0:T(8,128)(2,1)S(1)} %pad_maximum_fusion.6), channel_id=1, source_target_pairs={{0,4},{1,3},{2,6},{3,1},{4,0},{5,7},{6,2},{7,5},{8,12},{9,11},{10,... | collective-permute-start | bytes 1179656 | tf_op jit(solution)/shard_map/ppermute | solution.py:29
  97.0 8.5 %collective-permute-start.20 = (bf16[96,2048]{1,0:T(8,128)(2,1)S(1)}, bf16[96,2048]{1,0:T(8,128)(2,1)S(1)}, u32[]{:S(2)}, u32[]{:S(2)}) collective-permute-start(bf16[96,2048]{1,0:T(8,128)(2,1)S(1)} %pad_maximum_fusion.5), channel_id=1, source_target_pairs={{0,2},{1,5},{2,0},{3,7},{4,6},{5,1},{6,4},{7,3},{8,10},{9,13},{10,... | collective-permute-start | bytes 1179656 | tf_op jit(solution)/shard_map/ppermute | solution.py:29
  105.5 8.1 %collective-permute-start.25 = (bf16[64,2048]{1,0:T(8,128)(2,1)S(1)}, bf16[64,2048]{1,0:T(8,128)(2,1)S(1)}, u32[]{:S(2)}, u32[]{:S(2)}) collective-permute-start(bf16[64,2048]{1,0:T(8,128)(2,1)S(1)} %pad_maximum_fusion.9), channel_id=1, source_target_pairs={{0,2},{1,5},{2,0},{3,7},{4,6},{5,1},{6,4},{7,3},{8,10},{9,13},{10,... | collective-permute-start | bytes 786440 | tf_op jit(solution)/shard_map/ppermute | solution.py:29
  106.7 6.9 %collective-permute-start.26 = (bf16[64,2048]{1,0:T(8,128)(2,1)S(1)}, bf16[64,2048]{1,0:T(8,128)(2,1)S(1)}, u32[]{:S(2)}, u32[]{:S(2)}) collective-permute-start(bf16[64,2048]{1,0:T(8,128)(2,1)S(1)} %pad_maximum_fusion.10), channel_id=1, source_target_pairs={{0,4},{1,3},{2,6},{3,1},{4,0},{5,7},{6,2},{7,5},{8,12},{9,11},{10,... | collective-permute-start | bytes 786440 | tf_op jit(solution)/shard_map/ppermute | solution.py:29
  108.5 10.2 %collective-permute-start.22 = (bf16[64,2048]{1,0:T(8,128)(2,1)S(1)}, bf16[64,2048]{1,0:T(8,128)(2,1)S(1)}, u32[]{:S(2)}, u32[]{:S(2)}) collective-permute-start(bf16[64,2048]{1,0:T(8,128)(2,1)S(1)} %add_convert_fusion.1), channel_id=1, source_target_pairs={{0,24},{1,25},{2,26},{3,27},{4,28},{5,29},{6,30},{7,31},{8,16},{9,... | collective-permute-start | bytes 786440 | tf_op jit(solution)/shard_map/ppermute | solution.py:29
  110.1 24.5 %copy-start.1 = (bf16[128,1024]{1,0:T(8,128)(2,1)S(1)}, bf16[128,1024]{1,0:T(8,128)(2,1)}, u32[]{:S(2)}) copy-start(bf16[128,1024]{1,0:T(8,128)(2,1)} %param.9) | copy-start | bytes 786436
  113.7 9.1 %collective-permute-start.27 = (bf16[64,2048]{1,0:T(8,128)(2,1)S(1)}, bf16[64,2048]{1,0:T(8,128)(2,1)S(1)}, u32[]{:S(2)}, u32[]{:S(2)}) collective-permute-start(bf16[64,2048]{1,0:T(8,128)(2,1)S(1)} %fusion.8), channel_id=1, source_target_pairs={{0,8},{1,9},{2,10},{3,11},{4,12},{5,13},{6,14},{7,15},{24,16},{25,... | collective-permute-start | bytes 786440 | tf_op jit(solution)/shard_map/ppermute | solution.py:29
  118.7 6.4 %collective-permute-start.23 = (bf16[64,2048]{1,0:T(8,128)(2,1)S(1)}, bf16[64,2048]{1,0:T(8,128)(2,1)S(1)}, u32[]{:S(2)}, u32[]{:S(2)}) collective-permute-start(bf16[64,2048]{1,0:T(8,128)(2,1)S(1)} %pad_maximum_fusion.12), channel_id=1, source_target_pairs={{0,4},{1,3},{2,6},{3,1},{4,0},{5,7},{6,2},{7,5},{8,12},{9,11},{10,... | collective-permute-start | bytes 786440 | tf_op jit(solution)/shard_map/ppermute | solution.py:29
  120.8 6.4 %collective-permute-start.24 = (bf16[64,2048]{1,0:T(8,128)(2,1)S(1)}, bf16[64,2048]{1,0:T(8,128)(2,1)S(1)}, u32[]{:S(2)}, u32[]{:S(2)}) collective-permute-start(bf16[64,2048]{1,0:T(8,128)(2,1)S(1)} %pad_maximum_fusion.11), channel_id=1, source_target_pairs={{0,2},{1,5},{2,0},{3,7},{4,6},{5,1},{6,4},{7,3},{8,10},{9,13},{10,... | collective-permute-start | bytes 786440 | tf_op jit(solution)/shard_map/ppermute | solution.py:29
  122.9 4.9 %collective-permute-start.28 = (bf16[64,2048]{1,0:T(8,128)(2,1)S(1)}, bf16[64,2048]{1,0:T(8,128)(2,1)S(1)}, u32[]{:S(2)}, u32[]{:S(2)}) collective-permute-start(bf16[64,2048]{1,0:T(8,128)(2,1)S(1)} %add_convert_fusion), channel_id=1, source_target_pairs={{8,16},{9,17},{10,18},{11,19},{12,20},{13,21},{14,22},{15,23},{16,... | collective-permute-start | bytes 786440 | tf_op jit(solution)/shard_map/ppermute | solution.py:29
  127.3 6.4 %collective-permute-start.29 = (bf16[64,2048]{1,0:T(8,128)(2,1)S(1)}, bf16[64,2048]{1,0:T(8,128)(2,1)S(1)}, u32[]{:S(2)}, u32[]{:S(2)}) collective-permute-start(bf16[64,2048]{1,0:T(8,128)(2,1)S(1)} %fusion.7), channel_id=1, source_target_pairs={{0,8},{1,9},{2,10},{3,11},{4,12},{5,13},{6,14},{7,15},{8,0},{9,1},... | collective-permute-start | bytes 786440 | tf_op jit(solution)/shard_map/ppermute | solution.py:29
  (4 other events, 20.5 us)

commit v3 on v2

--- a/solution.py
+++ b/solution.py
@@ -212,7 +212,8 @@
             u = lax.dot_general(
                 x, ups[2 * i + 1, t], NT, preferred_element_type=jnp.float32
             )
-            acts[i, t] = (h / (1.0 + jnp.exp(-h)) * u).astype(jnp.bfloat16)
+            h = 0.5 * h
+            acts[i, t] = ((h + h * jnp.tanh(h)) * u).astype(jnp.bfloat16)
     if loads:
         for i in range(2):
             down_copy(i).wait()

time: 135 us -> 135 us (level)
  no operation moved by 1% of the time
where the time goes in v3:
time: 135 us
  waiting for transfers between devices  57.8 us (43%)
  starting transfers between devices  39.2 us (29%)
  Pallas kernels  23 us (17%)
  matrix products  6.38 us (5%)
  other arithmetic  4.93 us (4%)
  local copies, waits for them, and re-layouts  2.37 us (2%)
    ppermute x26, waiting for transfers between devices, send(): return lax.ppermute(value, ('req', 'tp'), pairs)  53.6 us
    ppermute x26, starting transfers between devices, send(): return lax.ppermute(value, ('req', 'tp'), pairs)  37.9 us
    pallas_call x2, Pallas kernels, run_experts(): pl.pallas_call(functools.partial(expert_body, takes, gives, tile, group,...  23 us
    dot_general x1, matrix products, project(): kept = jnp.dot(ours, out_weight, preferred_element_type=jnp.float32)  3.18 us
    dot_general x1, matrix products, project(): sent = jnp.dot(theirs, out_weight, preferred_element_type=jnp.float32)  3.07 us
  transfers between devices with their start and end apart: 30, of which 17 were waited for; matrix products, arithmetic and copies ran while one was open for 5% of the time, Pallas kernels for 17%

profile of v3, /device:TPU:0, one launch (start us, length us, event | category | flops | bytes accessed | tf_op | source)
XLA Modules:
  0.0 134.6 jit_solution(15737679694790534537)
XLA Ops:
  1.6 3.1 %fusion.10 = f32[64,2048]{1,0:T(8,128)S(1)} fusion(bf16[1024,2048]{1,0:T(8,128)(2,1)} %param.10, bf16[128,1024]{1,0:T(8,128)(2,1)S(1)} %copy-done, s32[]{:T(128)S(6)} %select_n.39), kind=kOutput, calls=%fused_computation.50 | convolution fusion | flops 268435456 | bytes 4849668 | tf_op jit(solution)/shard_map/dot_general | solution.py:303
  5.2 1.5 %collective-permute-done = f32[64,2048]{1,0:T(8,128)S(1)} collective-permute-done((f32[64,2048]{1,0:T(8,128)S(1)}, f32[64,2048]{1,0:T(8,128)S(1)}, u32[]{:S(2)}, u32[]{:S(2)}) %collective-permute-start) | collective-permute-done | bytes 524320 | tf_op jit(solution)/shard_map/ppermute | solution.py:304
  7.4 3.2 %fusion.12 = f32[64,2048]{1,0:T(8,128)S(1)} fusion(bf16[1024,2048]{1,0:T(8,128)(2,1)} %param.10, bf16[128,1024]{1,0:T(8,128)(2,1)S(1)} %copy-done, s32[]{:T(128)S(6)} %select_n.38), kind=kOutput, calls=%fused_computation.52 | convolution fusion | flops 268435456 | bytes 4849668 | tf_op jit(solution)/shard_map/dot_general | solution.py:305
  11.6 2.7 %collective-permute-done.1 = bf16[2,512,2048]{2,1,0:T(8,128)(2,1)} collective-permute-done((bf16[2,512,2048]{2,1,0:T(8,128)(2,1)}, bf16[2,512,2048]{2,1,0:T(8,128)(2,1)}, u32[]{:S(2)}, u32[]{:S(2)}) %collective-permute-start.1) | collective-permute-done | bytes 4194336 | tf_op jit(solution)/shard_map/ppermute | solution.py:56
  14.6 2.7 %collective-permute-start.5 = (bf16[64,2176]{1,0:T(8,128)(2,1)S(1)}, bf16[64,2176]{1,0:T(8,128)(2,1)S(1)}, u32[]{:S(2)}, u32[]{:S(2)}) collective-permute-start(bf16[64,2176]{1,0:T(8,128)(2,1)S(1)} %fusion.9.refs_0_), channel_id=1, source_target_pairs={{0,4},{1,3},{2,6},{3,1},{4,0},{5,7},{6,2},{7,5},{8,12},{9,11},{10,... | collective-permute-start | bytes 835592 | tf_op jit(solution)/shard_map/ppermute | solution.py:29
  17.3 1.5 %collective-permute-start.4 = (bf16[64,2176]{1,0:T(8,128)(2,1)S(1)}, bf16[64,2176]{1,0:T(8,128)(2,1)S(1)}, u32[]{:S(2)}, u32[]{:S(2)}) collective-permute-start(bf16[64,2176]{1,0:T(8,128)(2,1)S(1)} %fusion.9.refs_0_), channel_id=1, source_target_pairs={{0,2},{1,5},{2,0},{3,7},{4,6},{5,1},{6,4},{7,3},{8,10},{9,13},{10,... | collective-permute-start | bytes 835592 | tf_op jit(solution)/shard_map/ppermute | solution.py:29
  18.8 1.6 %collective-permute-start.3 = (bf16[64,2176]{1,0:T(8,128)(2,1)S(1)}, bf16[64,2176]{1,0:T(8,128)(2,1)S(1)}, u32[]{:S(2)}, u32[]{:S(2)}) collective-permute-start(bf16[64,2176]{1,0:T(8,128)(2,1)S(1)} %fusion.9.refs_0_), channel_id=1, source_target_pairs={{0,8},{1,9},{2,10},{3,11},{4,12},{5,13},{6,14},{7,15},{8,0},{9,1},... | collective-permute-start | bytes 835592 | tf_op jit(solution)/shard_map/ppermute | solution.py:29
  20.3 2.5 %collective-permute-start.2 = (bf16[64,2176]{1,0:T(8,128)(2,1)S(1)}, bf16[64,2176]{1,0:T(8,128)(2,1)S(1)}, u32[]{:S(2)}, u32[]{:S(2)}) collective-permute-start(bf16[64,2176]{1,0:T(8,128)(2,1)S(1)} %fusion.9.refs_0_), channel_id=1, source_target_pairs={{0,24},{1,25},{2,26},{3,27},{4,28},{5,29},{6,30},{7,31},{8,16},{9,... | collective-permute-start | bytes 835592 | tf_op jit(solution)/shard_map/ppermute | solution.py:29
  24.4 3.0 %collective-permute-done.3.refs_3_ = bf16[64,2176]{1,0:T(8,128)(2,1)S(1)} collective-permute-done((bf16[64,2176]{1,0:T(8,128)(2,1)S(1)}, bf16[64,2176]{1,0:T(8,128)(2,1)S(1)}, u32[]{:S(2)}, u32[]{:S(2)}) %collective-permute-start.3) | collective-permute-done | bytes 278560 | tf_op jit(solution)/shard_map/ppermute | solution.py:29
  27.4 7.8 %collective-permute-done.2 = bf16[64,2176]{1,0:T(8,128)(2,1)S(1)} collective-permute-done((bf16[64,2176]{1,0:T(8,128)(2,1)S(1)}, bf16[64,2176]{1,0:T(8,128)(2,1)S(1)}, u32[]{:S(2)}, u32[]{:S(2)}) %collective-permute-start.2) | collective-permute-done | bytes 278560 | tf_op jit(solution)/shard_map/ppermute | solution.py:29
  37.2 1.3 collective-permute-start.7
  38.4 1.4 %collective-permute-start.8 = (bf16[64,2176]{1,0:T(8,128)(2,1)S(1)}, bf16[64,2176]{1,0:T(8,128)(2,1)}, u32[]{:S(2)}, u32[]{:S(2)}) collective-permute-start(bf16[64,2176]{1,0:T(8,128)(2,1)S(1)} %collective-permute-done.3.refs_3_), channel_id=1, source_target_pairs={{8,16},{9,17},{10,18},{11,19},{12,20},{13,21},{14,22},{15,23},{16,... | collective-permute-start | bytes 835592 | tf_op jit(solution)/shard_map/ppermute | solution.py:29
  41.1 6.6 %collective-permute-done.7 = bf16[64,2176]{1,0:T(8,128)(2,1)} collective-permute-done((bf16[64,2176]{1,0:T(8,128)(2,1)S(1)}, bf16[64,2176]{1,0:T(8,128)(2,1)}, u32[]{:S(2)}, u32[]{:S(2)}) %collective-permute-start.7) | collective-permute-done | bytes 278560 | tf_op jit(solution)/shard_map/ppermute | solution.py:29
  50.4 1.5 %collective-permute-start.13 = (bf16[160,2176]{1,0:T(8,128)(2,1)S(1)}, bf16[160,2176]{1,0:T(8,128)(2,1)S(1)}, u32[]{:S(2)}, u32[]{:S(2)}) collective-permute-start(bf16[160,2176]{1,0:T(8,128)(2,1)S(1)} %get-tuple-element.91), channel_id=1, source_target_pairs={{0,4},{1,3},{2,6},{3,1},{4,0},{5,7},{6,2},{7,5},{8,12},{9,11},{10,... | collective-permute-start | bytes 2088968 | tf_op jit(solution)/shard_map/ppermute | solution.py:29
  51.9 13.2 %shard_map.104 = (bf16[64,2048]{1,0:T(8,128)(2,1)S(1)}, bf16[64,2048]{1,0:T(8,128)(2,1)S(1)}, bf16[64,2048]{1,0:T(8,128)(2,1)S(1)}, bf16[32,2048]{1,0:T(8,128)(2...) custom-call(bf16[64,2176]{1,0:T(8,128)(2,1)S(1)} %fusion.9.refs_0_, ...), custom_call_target="tpu_custom_call" | custom-call | flops 8589934592 | bytes 29360128 | tf_op jit(solution)/shard_map/pallas_call | solution.py:275
  65.1 2.6 %collective-permute-done.12.refs_0_ = bf16[160,2176]{1,0:T(8,128)(2,1)S(1)} collective-permute-done((bf16[160,2176]{1,0:T(8,128)(2,1)S(1)}, bf16[160,2176]{1,0:T(8,128)(2,1)S(1)}, u32[]{:S(2)}, u32[]{:S(2)}) %collective-permute-start.12) | collective-permute-done | bytes 696352 | tf_op jit(solution)/shard_map/ppermute | solution.py:29
  69.5 1.4 %collective-permute-start.14 = (bf16[96,2048]{1,0:T(8,128)(2,1)S(1)}, bf16[96,2048]{1,0:T(8,128)(2,1)S(1)}, u32[]{:S(2)}, u32[]{:S(2)}) collective-permute-start(bf16[96,2048]{1,0:T(8,128)(2,1)S(1)} %get-tuple-element.106), channel_id=1, source_target_pairs={{0,2},{1,5},{2,0},{3,7},{4,6},{5,1},{6,4},{7,3},{8,10},{9,13},{10,... | collective-permute-start | bytes 1179656 | tf_op jit(solution)/shard_map/ppermute | solution.py:29
  72.0 5.4 %collective-permute-done.16.refs_2_ = bf16[64,2176]{1,0:T(8,128)(2,1)S(1)} collective-permute-done((bf16[64,2176]{1,0:T(8,128)(2,1)S(1)}, bf16[64,2176]{1,0:T(8,128)(2,1)S(1)}, u32[]{:S(2)}, u32[]{:S(2)}) %collective-permute-start.16) | collective-permute-done | bytes 278560 | tf_op jit(solution)/shard_map/ppermute | solution.py:29
  78.4 9.8 %shard_map.105 = (bf16[64,2048]{1,0:T(8,128)(2,1)S(1)}, bf16[96,2048]{1,0:T(8,128)(2,1)S(1)}, bf16[64,2048]{1,0:T(8,128)(2,1)S(1)}, bf16[96,2048]{1,0:T(8,128)(2...) custom-call(bf16[160,2176]{1,0:T(8,128)(2,1)S(1)} %collective-permute-done.12.refs, ...), custom_call_target="tpu_custom_call" | custom-call | flops 8589934592 | bytes 29360128 | tf_op jit(solution)/shard_map/pallas_call | solution.py:275
  89.0 1.4 %collective-permute-start.19 = (bf16[64,2048]{1,0:T(8,128)(2,1)S(1)}, bf16[64,2048]{1,0:T(8,128)(2,1)S(1)}, u32[]{:S(2)}, u32[]{:S(2)}) collective-permute-start(bf16[64,2048]{1,0:T(8,128)(2,1)S(1)} %get-tuple-element.127), channel_id=1, source_target_pairs={{0,2},{1,5},{2,0},{3,7},{4,6},{5,1},{6,4},{7,3},{8,10},{9,13},{10,... | collective-permute-start | bytes 786440 | tf_op jit(solution)/shard_map/ppermute | solution.py:29
  90.5 4.9 %collective-permute-done.19 = bf16[64,2048]{1,0:T(8,128)(2,1)S(1)} collective-permute-done((bf16[64,2048]{1,0:T(8,128)(2,1)S(1)}, bf16[64,2048]{1,0:T(8,128)(2,1)S(1)}, u32[]{:S(2)}, u32[]{:S(2)}) %collective-permute-start.19) | collective-permute-done | bytes 262176 | tf_op jit(solution)/shard_map/ppermute | solution.py:29
  95.5 1.4 %collective-permute-start.21 = (bf16[96,2048]{1,0:T(8,128)(2,1)S(1)}, bf16[96,2048]{1,0:T(8,128)(2,1)S(1)}, u32[]{:S(2)}, u32[]{:S(2)}) collective-permute-start(bf16[96,2048]{1,0:T(8,128)(2,1)S(1)} %pad_maximum_fusion.6), channel_id=1, source_target_pairs={{0,4},{1,3},{2,6},{3,1},{4,0},{5,7},{6,2},{7,5},{8,12},{9,11},{10,... | collective-permute-start | bytes 1179656 | tf_op jit(solution)/shard_map/ppermute | solution.py:29
  98.3 7.2 %collective-permute-done.21 = bf16[96,2048]{1,0:T(8,128)(2,1)S(1)} collective-permute-done((bf16[96,2048]{1,0:T(8,128)(2,1)S(1)}, bf16[96,2048]{1,0:T(8,128)(2,1)S(1)}, u32[]{:S(2)}, u32[]{:S(2)}) %collective-permute-start.21) | collective-permute-done | bytes 393248 | tf_op jit(solution)/shard_map/ppermute | solution.py:29
  106.7 1.7 %collective-permute-start.26 = (bf16[64,2048]{1,0:T(8,128)(2,1)S(1)}, bf16[64,2048]{1,0:T(8,128)(2,1)S(1)}, u32[]{:S(2)}, u32[]{:S(2)}) collective-permute-start(bf16[64,2048]{1,0:T(8,128)(2,1)S(1)} %pad_maximum_fusion.10), channel_id=1, source_target_pairs={{0,4},{1,3},{2,6},{3,1},{4,0},{5,7},{6,2},{7,5},{8,12},{9,11},{10,... | collective-permute-start | bytes 786440 | tf_op jit(solution)/shard_map/ppermute | solution.py:29
  108.5 1.5 %collective-permute-start.22 = (bf16[64,2048]{1,0:T(8,128)(2,1)S(1)}, bf16[64,2048]{1,0:T(8,128)(2,1)S(1)}, u32[]{:S(2)}, u32[]{:S(2)}) collective-permute-start(bf16[64,2048]{1,0:T(8,128)(2,1)S(1)} %add_convert_fusion.1), channel_id=1, source_target_pairs={{0,24},{1,25},{2,26},{3,27},{4,28},{5,29},{6,30},{7,31},{8,16},{9,... | collective-permute-start | bytes 786440 | tf_op jit(solution)/shard_map/ppermute | solution.py:29
  110.1 3.4 %collective-permute-done.25 = bf16[64,2048]{1,0:T(8,128)(2,1)S(1)} collective-permute-done((bf16[64,2048]{1,0:T(8,128)(2,1)S(1)}, bf16[64,2048]{1,0:T(8,128)(2,1)S(1)}, u32[]{:S(2)}, u32[]{:S(2)}) %collective-permute-start.25) | collective-permute-done | bytes 262176 | tf_op jit(solution)/shard_map/ppermute | solution.py:29
  113.7 4.9 %collective-permute-start.27 = (bf16[64,2048]{1,0:T(8,128)(2,1)S(1)}, bf16[64,2048]{1,0:T(8,128)(2,1)S(1)}, u32[]{:S(2)}, u32[]{:S(2)}) collective-permute-start(bf16[64,2048]{1,0:T(8,128)(2,1)S(1)} %fusion.8), channel_id=1, source_target_pairs={{0,8},{1,9},{2,10},{3,11},{4,12},{5,13},{6,14},{7,15},{24,16},{25,... | collective-permute-start | bytes 786440 | tf_op jit(solution)/shard_map/ppermute | solution.py:29
  118.7 2.1 %collective-permute-start.23 = (bf16[64,2048]{1,0:T(8,128)(2,1)S(1)}, bf16[64,2048]{1,0:T(8,128)(2,1)S(1)}, u32[]{:S(2)}, u32[]{:S(2)}) collective-permute-start(bf16[64,2048]{1,0:T(8,128)(2,1)S(1)} %pad_maximum_fusion.12), channel_id=1, source_target_pairs={{0,4},{1,3},{2,6},{3,1},{4,0},{5,7},{6,2},{7,5},{8,12},{9,11},{10,... | collective-permute-start | bytes 786440 | tf_op jit(solution)/shard_map/ppermute | solution.py:29
  120.7 2.0 %collective-permute-start.24 = (bf16[64,2048]{1,0:T(8,128)(2,1)S(1)}, bf16[64,2048]{1,0:T(8,128)(2,1)S(1)}, u32[]{:S(2)}, u32[]{:S(2)}) collective-permute-start(bf16[64,2048]{1,0:T(8,128)(2,1)S(1)} %pad_maximum_fusion.11), channel_id=1, source_target_pairs={{0,2},{1,5},{2,0},{3,7},{4,6},{5,1},{6,4},{7,3},{8,10},{9,13},{10,... | collective-permute-start | bytes 786440 | tf_op jit(solution)/shard_map/ppermute | solution.py:29
  123.6 1.5 %collective-permute-done.23 = bf16[64,2048]{1,0:T(8,128)(2,1)S(1)} collective-permute-done((bf16[64,2048]{1,0:T(8,128)(2,1)S(1)}, bf16[64,2048]{1,0:T(8,128)(2,1)S(1)}, u32[]{:S(2)}, u32[]{:S(2)}) %collective-permute-start.23) | collective-permute-done | bytes 262176 | tf_op jit(solution)/shard_map/ppermute | solution.py:29
  125.2 1.9 %collective-permute-done.24 = bf16[64,2048]{1,0:T(8,128)(2,1)S(1)} collective-permute-done((bf16[64,2048]{1,0:T(8,128)(2,1)S(1)}, bf16[64,2048]{1,0:T(8,128)(2,1)S(1)}, u32[]{:S(2)}, u32[]{:S(2)}) %collective-permute-start.24) | collective-permute-done | bytes 262176 | tf_op jit(solution)/shard_map/ppermute | solution.py:29
  127.8 5.9 %collective-permute-done.29 = bf16[64,2048]{1,0:T(8,128)(2,1)S(1)} collective-permute-done((bf16[64,2048]{1,0:T(8,128)(2,1)S(1)}, bf16[64,2048]{1,0:T(8,128)(2,1)S(1)}, u32[]{:S(2)}, u32[]{:S(2)}) %collective-permute-start.29) | collective-permute-done | bytes 262176 | tf_op jit(solution)/shard_map/ppermute | solution.py:29
  (87 shorter events, 21.1 us)
Async XLA Ops:
  1.6 9.0 %copy-start.2 = (bf16[64,2048]{1,0:T(8,128)(2,1)S(1)}, bf16[64,2048]{1,0:T(8,128)(2,1)}, u32[]{:S(2)}) copy-start(bf16[64,2048]{1,0:T(8,128)(2,1)} %param.11) | copy-start | bytes 786436
  4.7 2.1 %collective-permute-start = (f32[64,2048]{1,0:T(8,128)S(1)}, f32[64,2048]{1,0:T(8,128)S(1)}, u32[]{:S(2)}, u32[]{:S(2)}) collective-permute-start(f32[64,2048]{1,0:T(8,128)S(1)} %fusion.10), channel_id=1, source_target_pairs={{0,1},{1,0},{2,3},{3,2},{4,5},{5,4},{6,7},{7,6},{8,9},{9,8},{10,11... | collective-permute-start | bytes 1572872 | tf_op jit(solution)/shard_map/ppermute | solution.py:304
  6.7 7.5 %collective-permute-start.1 = (bf16[2,512,2048]{2,1,0:T(8,128)(2,1)}, bf16[2,512,2048]{2,1,0:T(8,128)(2,1)}, u32[]{:S(2)}, u32[]{:S(2)}) collective-permute-start(bf16[2,512,2048]{2,1,0:T(8,128)(2,1)} %param.15), channel_id=1, source_target_pairs={{0,1},{1,0},{2,3},{3,2},{4,5},{5,4},{6,7},{7,6},{8,9},{9,8},{10,11... | collective-permute-start | bytes 12582920 | tf_op jit(solution)/shard_map/ppermute | solution.py:56
  14.2 21.0 %collective-permute-start.6 = (bf16[2,512,2048]{2,1,0:T(8,128)(2,1)S(1)}, bf16[2,512,2048]{2,1,0:T(8,128)(2,1)}, u32[]{:S(2)}, u32[]{:S(2)}) collective-permute-start(bf16[2,512,2048]{2,1,0:T(8,128)(2,1)S(1)} %copy-done.5), channel_id=1, source_target_pairs={{0,1},{1,0},{2,3},{3,2},{4,5},{5,4},{6,7},{7,6},{8,9},{9,8},{10,11... | collective-permute-start | bytes 12582920 | tf_op jit(solution)/shard_map/ppermute | solution.py:56
  14.6 9.1 %collective-permute-start.5 = (bf16[64,2176]{1,0:T(8,128)(2,1)S(1)}, bf16[64,2176]{1,0:T(8,128)(2,1)S(1)}, u32[]{:S(2)}, u32[]{:S(2)}) collective-permute-start(bf16[64,2176]{1,0:T(8,128)(2,1)S(1)} %fusion.9.refs_0_), channel_id=1, source_target_pairs={{0,4},{1,3},{2,6},{3,1},{4,0},{5,7},{6,2},{7,5},{8,12},{9,11},{10,... | collective-permute-start | bytes 835592 | tf_op jit(solution)/shard_map/ppermute | solution.py:29
  17.3 7.2 %collective-permute-start.4 = (bf16[64,2176]{1,0:T(8,128)(2,1)S(1)}, bf16[64,2176]{1,0:T(8,128)(2,1)S(1)}, u32[]{:S(2)}, u32[]{:S(2)}) collective-permute-start(bf16[64,2176]{1,0:T(8,128)(2,1)S(1)} %fusion.9.refs_0_), channel_id=1, source_target_pairs={{0,2},{1,5},{2,0},{3,7},{4,6},{5,1},{6,4},{7,3},{8,10},{9,13},{10,... | collective-permute-start | bytes 835592 | tf_op jit(solution)/shard_map/ppermute | solution.py:29
  18.8 8.6 %collective-permute-start.3 = (bf16[64,2176]{1,0:T(8,128)(2,1)S(1)}, bf16[64,2176]{1,0:T(8,128)(2,1)S(1)}, u32[]{:S(2)}, u32[]{:S(2)}) collective-permute-start(bf16[64,2176]{1,0:T(8,128)(2,1)S(1)} %fusion.9.refs_0_), channel_id=1, source_target_pairs={{0,8},{1,9},{2,10},{3,11},{4,12},{5,13},{6,14},{7,15},{8,0},{9,1},... | collective-permute-start | bytes 835592 | tf_op jit(solution)/shard_map/ppermute | solution.py:29
  20.3 14.9 %collective-permute-start.2 = (bf16[64,2176]{1,0:T(8,128)(2,1)S(1)}, bf16[64,2176]{1,0:T(8,128)(2,1)S(1)}, u32[]{:S(2)}, u32[]{:S(2)}) collective-permute-start(bf16[64,2176]{1,0:T(8,128)(2,1)S(1)} %fusion.9.refs_0_), channel_id=1, source_target_pairs={{0,24},{1,25},{2,26},{3,27},{4,28},{5,29},{6,30},{7,31},{8,16},{9,... | collective-permute-start | bytes 835592 | tf_op jit(solution)/shard_map/ppermute | solution.py:29
  36.1 12.3 %collective-permute-start.11 = (bf16[2,512,2048]{2,1,0:T(8,128)(2,1)}, bf16[2,512,2048]{2,1,0:T(8,128)(2,1)}, u32[]{:S(2)}, u32[]{:S(2)}) collective-permute-start(bf16[2,512,2048]{2,1,0:T(8,128)(2,1)} %param.17), channel_id=1, source_target_pairs={{0,1},{1,0},{2,3},{3,2},{4,5},{5,4},{6,7},{7,6},{8,9},{9,8},{10,11... | collective-permute-start | bytes 12582920 | tf_op jit(solution)/shard_map/ppermute | solution.py:56
  36.1 12.3 %collective-permute-start.9 = (bf16[96,2176]{1,0:T(8,128)(2,1)}, bf16[96,2176]{1,0:T(8,128)(2,1)S(1)}, u32[]{:S(2)}, u32[]{:S(2)}) collective-permute-start(bf16[96,2176]{1,0:T(8,128)(2,1)} %get-tuple-element.83), channel_id=1, source_target_pairs={{0,2},{1,5},{2,0},{3,7},{4,6},{5,1},{6,4},{7,3},{8,10},{9,13},{10,... | collective-permute-start | bytes 1253384 | tf_op jit(solution)/shard_map/ppermute | solution.py:29
  36.6 11.7 %collective-permute-start.10 = (bf16[96,2176]{1,0:T(8,128)(2,1)S(1)}, bf16[96,2176]{1,0:T(8,128)(2,1)S(1)}, u32[]{:S(2)}, u32[]{:S(2)}) collective-permute-start(bf16[96,2176]{1,0:T(8,128)(2,1)S(1)} %get-tuple-element.84), channel_id=1, source_target_pairs={{0,4},{1,3},{2,6},{3,1},{4,0},{5,7},{6,2},{7,5},{8,12},{9,11},{10,... | collective-permute-start | bytes 1253384 | tf_op jit(solution)/shard_map/ppermute | solution.py:29
  37.2 10.5 %collective-permute-start.7 = (bf16[64,2176]{1,0:T(8,128)(2,1)S(1)}, bf16[64,2176]{1,0:T(8,128)(2,1)}, u32[]{:S(2)}, u32[]{:S(2)}) collective-permute-start(bf16[64,2176]{1,0:T(8,128)(2,1)S(1)} %collective-permute-done.2), channel_id=1, source_target_pairs={{8,0},{9,1},{10,2},{11,3},{12,4},{13,5},{14,6},{15,7},{16,24},{17,... | collective-permute-start | bytes 835592 | tf_op jit(solution)/shard_map/ppermute | solution.py:29
  38.4 9.2 %collective-permute-start.8 = (bf16[64,2176]{1,0:T(8,128)(2,1)S(1)}, bf16[64,2176]{1,0:T(8,128)(2,1)}, u32[]{:S(2)}, u32[]{:S(2)}) collective-permute-start(bf16[64,2176]{1,0:T(8,128)(2,1)S(1)} %collective-permute-done.3.refs_3_), channel_id=1, source_target_pairs={{8,16},{9,17},{10,18},{11,19},{12,20},{13,21},{14,22},{15,23},{16,... | collective-permute-start | bytes 835592 | tf_op jit(solution)/shard_map/ppermute | solution.py:29
  49.6 18.2 %collective-permute-start.12 = (bf16[160,2176]{1,0:T(8,128)(2,1)S(1)}, bf16[160,2176]{1,0:T(8,128)(2,1)S(1)}, u32[]{:S(2)}, u32[]{:S(2)}) collective-permute-start(bf16[160,2176]{1,0:T(8,128)(2,1)S(1)} %get-tuple-element.90), channel_id=1, source_target_pairs={{0,2},{1,5},{2,0},{3,7},{4,6},{5,1},{6,4},{7,3},{8,10},{9,13},{10,... | collective-permute-start | bytes 2088968 | tf_op jit(solution)/shard_map/ppermute | solution.py:29
  50.4 17.4 %collective-permute-start.13 = (bf16[160,2176]{1,0:T(8,128)(2,1)S(1)}, bf16[160,2176]{1,0:T(8,128)(2,1)S(1)}, u32[]{:S(2)}, u32[]{:S(2)}) collective-permute-start(bf16[160,2176]{1,0:T(8,128)(2,1)S(1)} %get-tuple-element.91), channel_id=1, source_target_pairs={{0,4},{1,3},{2,6},{3,1},{4,0},{5,7},{6,2},{7,5},{8,12},{9,11},{10,... | collective-permute-start | bytes 2088968 | tf_op jit(solution)/shard_map/ppermute | solution.py:29
  67.9 9.5 %collective-permute-start.16 = (bf16[64,2176]{1,0:T(8,128)(2,1)S(1)}, bf16[64,2176]{1,0:T(8,128)(2,1)S(1)}, u32[]{:S(2)}, u32[]{:S(2)}) collective-permute-start(bf16[64,2176]{1,0:T(8,128)(2,1)S(1)} %pad_maximum_fusion.7), channel_id=1, source_target_pairs={{0,2},{1,5},{2,0},{3,7},{4,6},{5,1},{6,4},{7,3},{8,10},{9,13},{10,... | collective-permute-start | bytes 835592 | tf_op jit(solution)/shard_map/ppermute | solution.py:29
  68.8 9.6 %collective-permute-start.17 = (bf16[64,2176]{1,0:T(8,128)(2,1)S(1)}, bf16[64,2176]{1,0:T(8,128)(2,1)S(1)}, u32[]{:S(2)}, u32[]{:S(2)}) collective-permute-start(bf16[64,2176]{1,0:T(8,128)(2,1)S(1)} %pad_maximum_fusion.8), channel_id=1, source_target_pairs={{0,4},{1,3},{2,6},{3,1},{4,0},{5,7},{6,2},{7,5},{8,12},{9,11},{10,... | collective-permute-start | bytes 835592 | tf_op jit(solution)/shard_map/ppermute | solution.py:29
  69.5 18.7 %collective-permute-start.14 = (bf16[96,2048]{1,0:T(8,128)(2,1)S(1)}, bf16[96,2048]{1,0:T(8,128)(2,1)S(1)}, u32[]{:S(2)}, u32[]{:S(2)}) collective-permute-start(bf16[96,2048]{1,0:T(8,128)(2,1)S(1)} %get-tuple-element.106), channel_id=1, source_target_pairs={{0,2},{1,5},{2,0},{3,7},{4,6},{5,1},{6,4},{7,3},{8,10},{9,13},{10,... | collective-permute-start | bytes 1179656 | tf_op jit(solution)/shard_map/ppermute | solution.py:29
  70.9 17.3 %collective-permute-start.15 = (bf16[96,2048]{1,0:T(8,128)(2,1)S(1)}, bf16[96,2048]{1,0:T(8,128)(2,1)S(1)}, u32[]{:S(2)}, u32[]{:S(2)}) collective-permute-start(bf16[96,2048]{1,0:T(8,128)(2,1)S(1)} %get-tuple-element.107), channel_id=1, source_target_pairs={{0,4},{1,3},{2,6},{3,1},{4,0},{5,7},{6,2},{7,5},{8,12},{9,11},{10,... | collective-permute-start | bytes 1179656 | tf_op jit(solution)/shard_map/ppermute | solution.py:29
  88.2 8.6 %collective-permute-start.18 = (bf16[64,2048]{1,0:T(8,128)(2,1)S(1)}, bf16[64,2048]{1,0:T(8,128)(2,1)S(1)}, u32[]{:S(2)}, u32[]{:S(2)}) collective-permute-start(bf16[64,2048]{1,0:T(8,128)(2,1)S(1)} %get-tuple-element.125), channel_id=1, source_target_pairs={{0,4},{1,3},{2,6},{3,1},{4,0},{5,7},{6,2},{7,5},{8,12},{9,11},{10,... | collective-permute-start | bytes 786440 | tf_op jit(solution)/shard_map/ppermute | solution.py:29
  89.0 6.4 %collective-permute-start.19 = (bf16[64,2048]{1,0:T(8,128)(2,1)S(1)}, bf16[64,2048]{1,0:T(8,128)(2,1)S(1)}, u32[]{:S(2)}, u32[]{:S(2)}) collective-permute-start(bf16[64,2048]{1,0:T(8,128)(2,1)S(1)} %get-tuple-element.127), channel_id=1, source_target_pairs={{0,2},{1,5},{2,0},{3,7},{4,6},{5,1},{6,4},{7,3},{8,10},{9,13},{10,... | collective-permute-start | bytes 786440 | tf_op jit(solution)/shard_map/ppermute | solution.py:29
  95.5 10.0 %collective-permute-start.21 = (bf16[96,2048]{1,0:T(8,128)(2,1)S(1)}, bf16[96,2048]{1,0:T(8,128)(2,1)S(1)}, u32[]{:S(2)}, u32[]{:S(2)}) collective-permute-start(bf16[96,2048]{1,0:T(8,128)(2,1)S(1)} %pad_maximum_fusion.6), channel_id=1, source_target_pairs={{0,4},{1,3},{2,6},{3,1},{4,0},{5,7},{6,2},{7,5},{8,12},{9,11},{10,... | collective-permute-start | bytes 1179656 | tf_op jit(solution)/shard_map/ppermute | solution.py:29
  97.0 8.5 %collective-permute-start.20 = (bf16[96,2048]{1,0:T(8,128)(2,1)S(1)}, bf16[96,2048]{1,0:T(8,128)(2,1)S(1)}, u32[]{:S(2)}, u32[]{:S(2)}) collective-permute-start(bf16[96,2048]{1,0:T(8,128)(2,1)S(1)} %pad_maximum_fusion.5), channel_id=1, source_target_pairs={{0,2},{1,5},{2,0},{3,7},{4,6},{5,1},{6,4},{7,3},{8,10},{9,13},{10,... | collective-permute-start | bytes 1179656 | tf_op jit(solution)/shard_map/ppermute | solution.py:29
  105.5 8.1 %collective-permute-start.25 = (bf16[64,2048]{1,0:T(8,128)(2,1)S(1)}, bf16[64,2048]{1,0:T(8,128)(2,1)S(1)}, u32[]{:S(2)}, u32[]{:S(2)}) collective-permute-start(bf16[64,2048]{1,0:T(8,128)(2,1)S(1)} %pad_maximum_fusion.9), channel_id=1, source_target_pairs={{0,2},{1,5},{2,0},{3,7},{4,6},{5,1},{6,4},{7,3},{8,10},{9,13},{10,... | collective-permute-start | bytes 786440 | tf_op jit(solution)/shard_map/ppermute | solution.py:29
  106.7 6.9 %collective-permute-start.26 = (bf16[64,2048]{1,0:T(8,128)(2,1)S(1)}, bf16[64,2048]{1,0:T(8,128)(2,1)S(1)}, u32[]{:S(2)}, u32[]{:S(2)}) collective-permute-start(bf16[64,2048]{1,0:T(8,128)(2,1)S(1)} %pad_maximum_fusion.10), channel_id=1, source_target_pairs={{0,4},{1,3},{2,6},{3,1},{4,0},{5,7},{6,2},{7,5},{8,12},{9,11},{10,... | collective-permute-start | bytes 786440 | tf_op jit(solution)/shard_map/ppermute | solution.py:29
  108.5 10.1 %collective-permute-start.22 = (bf16[64,2048]{1,0:T(8,128)(2,1)S(1)}, bf16[64,2048]{1,0:T(8,128)(2,1)S(1)}, u32[]{:S(2)}, u32[]{:S(2)}) collective-permute-start(bf16[64,2048]{1,0:T(8,128)(2,1)S(1)} %add_convert_fusion.1), channel_id=1, source_target_pairs={{0,24},{1,25},{2,26},{3,27},{4,28},{5,29},{6,30},{7,31},{8,16},{9,... | collective-permute-start | bytes 786440 | tf_op jit(solution)/shard_map/ppermute | solution.py:29
  110.1 24.5 %copy-start.1 = (bf16[128,1024]{1,0:T(8,128)(2,1)S(1)}, bf16[128,1024]{1,0:T(8,128)(2,1)}, u32[]{:S(2)}) copy-start(bf16[128,1024]{1,0:T(8,128)(2,1)} %param.9) | copy-start | bytes 786436
  113.7 9.1 %collective-permute-start.27 = (bf16[64,2048]{1,0:T(8,128)(2,1)S(1)}, bf16[64,2048]{1,0:T(8,128)(2,1)S(1)}, u32[]{:S(2)}, u32[]{:S(2)}) collective-permute-start(bf16[64,2048]{1,0:T(8,128)(2,1)S(1)} %fusion.8), channel_id=1, source_target_pairs={{0,8},{1,9},{2,10},{3,11},{4,12},{5,13},{6,14},{7,15},{24,16},{25,... | collective-permute-start | bytes 786440 | tf_op jit(solution)/shard_map/ppermute | solution.py:29
  118.7 6.4 %collective-permute-start.23 = (bf16[64,2048]{1,0:T(8,128)(2,1)S(1)}, bf16[64,2048]{1,0:T(8,128)(2,1)S(1)}, u32[]{:S(2)}, u32[]{:S(2)}) collective-permute-start(bf16[64,2048]{1,0:T(8,128)(2,1)S(1)} %pad_maximum_fusion.12), channel_id=1, source_target_pairs={{0,4},{1,3},{2,6},{3,1},{4,0},{5,7},{6,2},{7,5},{8,12},{9,11},{10,... | collective-permute-start | bytes 786440 | tf_op jit(solution)/shard_map/ppermute | solution.py:29
  120.7 6.4 %collective-permute-start.24 = (bf16[64,2048]{1,0:T(8,128)(2,1)S(1)}, bf16[64,2048]{1,0:T(8,128)(2,1)S(1)}, u32[]{:S(2)}, u32[]{:S(2)}) collective-permute-start(bf16[64,2048]{1,0:T(8,128)(2,1)S(1)} %pad_maximum_fusion.11), channel_id=1, source_target_pairs={{0,2},{1,5},{2,0},{3,7},{4,6},{5,1},{6,4},{7,3},{8,10},{9,13},{10,... | collective-permute-start | bytes 786440 | tf_op jit(solution)/shard_map/ppermute | solution.py:29
  122.9 4.9 %collective-permute-start.28 = (bf16[64,2048]{1,0:T(8,128)(2,1)S(1)}, bf16[64,2048]{1,0:T(8,128)(2,1)S(1)}, u32[]{:S(2)}, u32[]{:S(2)}) collective-permute-start(bf16[64,2048]{1,0:T(8,128)(2,1)S(1)} %add_convert_fusion), channel_id=1, source_target_pairs={{8,16},{9,17},{10,18},{11,19},{12,20},{13,21},{14,22},{15,23},{16,... | collective-permute-start | bytes 786440 | tf_op jit(solution)/shard_map/ppermute | solution.py:29
  127.3 6.4 %collective-permute-start.29 = (bf16[64,2048]{1,0:T(8,128)(2,1)S(1)}, bf16[64,2048]{1,0:T(8,128)(2,1)S(1)}, u32[]{:S(2)}, u32[]{:S(2)}) collective-permute-start(bf16[64,2048]{1,0:T(8,128)(2,1)S(1)} %fusion.7), channel_id=1, source_target_pairs={{0,8},{1,9},{2,10},{3,11},{4,12},{5,13},{6,14},{7,15},{8,0},{9,1},... | collective-permute-start | bytes 786440 | tf_op jit(solution)/shard_map/ppermute | solution.py:29
  (4 other events, 20.5 us)
